TPU v7x, 256 devices: a whole 4x4x8 slice. The times are simulated.
256 devices in a mesh: rows: 8 (over y, core), cols: 32 (over x, z).
Axes of the slice: x: 4, y: 4, z: 8, core: 2. Of those that a mesh axis runs over, the one named last changes fastest.
Arguments:
- logged: bfloat16 [32768, 128], P(('rows', 'cols')), may hold values from -5 to 5
- targets: bfloat16 [65536, 128], P('cols'), may hold values from -5 to 5
- log_a: float32 [32768], P('rows'), may hold values from -2 to 2
- log_b: float32 [65536], P('cols'), may hold values from -2 to 2
- start_g: float32 [65536], P('cols'), may hold values from -2 to 142
Outputs:
- pot_f: float32 [32768], P('rows')
- pot_g: float32 [65536], P('cols')
All inputs are finite; a program needn't handle non-finite values.
Results may differ from a plain program's by a relative error of at most 0.0003.
Values may be sent and summed in bfloat16 or wider, within the bound.
A program may use at most 64 MiB of HBM per device.

v0:
```python
import jax
import jax.numpy as jnp
from jax import lax
from jax.sharding import PartitionSpec as P

ITERS = 3


EPS = 0.5
BLOCK = 256


def inner_cost(xb, targets, tnorm):
    xnorm = jnp.sum(jnp.square(xb.astype(jnp.float32)), axis=1)
    inner = lax.dot_general(
        xb, targets, (((1,), (1,)), ((), ())), preferred_element_type=jnp.float32
    )
    return xnorm[:, None] + tnorm[None, :] - 2.0 * inner


def row_partial(x_piece, targets, tnorm, log_b, pot_g):

    def one(xb):
        cost = inner_cost(xb, targets, tnorm)
        s = log_b[None, :] + (pot_g[None, :] - cost) / EPS
        top = jnp.max(s, axis=1)
        total = jnp.sum(jnp.exp(s - top[:, None]), axis=1)
        return jnp.stack([top, total])

    count = x_piece.shape[0]
    parts = lax.map(one, x_piece.reshape(count // BLOCK, BLOCK, x_piece.shape[1]))
    return jnp.transpose(parts, (1, 0, 2)).reshape(2, count)


def col_update(carry, x_piece, f_piece, a_piece, targets, tnorm):

    def step(state, item):
        xb, fb, ab = item
        cost = inner_cost(xb, targets, tnorm)
        s = ab[:, None] + (fb[:, None] - cost) / EPS
        upper = jnp.maximum(state[0], jnp.max(s, axis=0))
        total = state[1] * jnp.exp(state[0] - upper) + jnp.sum(jnp.exp(s - upper[None, :]), axis=0)
        return ((upper, total), None)

    count = x_piece.shape[0]
    blocks = count // BLOCK
    items = (
        x_piece.reshape(blocks, BLOCK, x_piece.shape[1]),
        f_piece.reshape(blocks, BLOCK),
        a_piece.reshape(blocks, BLOCK),
    )
    result, unused = lax.scan(step, carry, items)
    return result


def join_cols(top, total):
    upper = lax.pmax(top, "cols")
    whole = lax.psum(total * jnp.exp(top - upper), "cols")
    return -EPS * (upper + jnp.log(whole))


def join_rows(top, total):
    upper = lax.pmax(top, "rows")
    whole = lax.psum(total * jnp.exp(top - upper), "rows")
    return -EPS * (upper + jnp.log(whole))


def local(logged, targets, log_a, log_b, start_g):
    tnorm = jnp.sum(jnp.square(targets.astype(jnp.float32)), axis=1)
    width = targets.shape[0]
    pot_g = start_g
    pot_f = jnp.zeros(log_a.shape, jnp.float32)
    gathered = lax.all_gather(logged, "cols", axis=0, tiled=True)
    for step in range(ITERS):
        partial_value = row_partial(gathered, targets, tnorm, log_b, pot_g)
        pot_f = join_cols(partial_value[0], partial_value[1])
        init = (jnp.full((width,), -1e30, jnp.float32), jnp.zeros((width,), jnp.float32))
        top, total = col_update(init, gathered, pot_f, log_a, targets, tnorm)
        pot_g = join_rows(top, total)
    return (pot_f, pot_g)


def solution(mesh):
    placed = (P(("rows", "cols"), None), P("cols", None), P("rows"), P("cols"), P("cols"))
    return jax.shard_map(
        local, mesh=mesh, in_specs=placed, out_specs=(P("rows"), P("cols")), check_vma=False
    )
```

profile of v0, /device:TPU:1, one launch (start us, length us, event | category | flops | bytes accessed | tf_op | source)
XLA Modules:
  0.0 1307.4 jit_solution(6303000346675965485)
XLA Ops:
  10.1 76.1 %all-gather.2.cloned.1.call-done = bf16[4096,128]{1,0:T(8,128)(2,1)} async-done(((bf16[128,128]{1,0:T(8,128)(2,1)}), bf16[4096,128]{1,0:T(8,128)(2,1)}) %all-gather.2.cloned.1.call-update) | async-done | bytes 1048592 | tf_op jit(solution)/shard_map/all_gather | solution.py:73
  86.2 51.2 %while.69 = (s32[]{:T(128)}, f32[16,2,256]{2,1,0:T(2,128)S(1)}, f32[2048]{0:T(1024)}, f32[2048]{0:T(1024)}, bf16[16,256,128]{2,1,0:T(8,128)(2,1)}, /*index=5*/f3...) while((s32[]{:T(128)}, f32[16,2,256]{2,1,0:T(2,128)S(1)}, f32[2048]{0:T(1024)}, f32[2048]{0:T(1024)}, ...), condition=%wide.region_5.6_spmd, body=%wide.region_1.5_spmd.sunk | while | flops 139034368 | bytes 4884061 | solution.py:31
  137.4 112.5 %pmax.42 = f32[4096]{0:T(1024)S(1)} all-reduce(f32[4096]{0:T(1024)S(1)} %bitcast.143), channel_id=1, replica_groups=mesh['rows'=8,'cols'=32] {'cols'}, use_global_device_ids=true, to_apply=%region_6.7 | all-reduce | flops 4096 | bytes 32768 | tf_op jit(solution)/shard_map/pmax | solution.py:57
  249.9 110.6 %psum.42 = f32[4096]{0:T(1024)S(1)} all-reduce(f32[4096]{0:T(1024)S(1)} %exponential_multiply_fusion.2), channel_id=1, replica_groups=mesh['rows'=8,'cols'=32] {'cols'}, use_global_device_ids=true, to_apply=%region_7.8 | all-reduce | flops 4096 | bytes 32768 | tf_op jit(solution)/shard_map/psum | solution.py:58
  360.5 49.6 %while.72 = (s32[]{:T(128)}, f32[2048]{0:T(1024)S(1)}, f32[2048]{0:T(1024)S(1)}, f32[16,256]{1,0:T(8,128)S(1)}, f32[16,256]{1,0:T(8,128)S(1)}, /*index=5*/bf16[1...) while((s32[]{:T(128)}, f32[2048]{0:T(1024)S(1)}, ...), condition=%wide.region_12.13_spmd.clone, body=%wide.region_8.12_spmd.clone.sunk | while | flops 139044608 | bytes 4973176 | solution.py:52
  410.1 72.0 %pmax.43 = f32[2048]{0:T(1024)S(1)} all-reduce(f32[2048]{0:T(1024)S(1)} %get-tuple-element.243), channel_id=1, replica_groups=mesh['rows'=8,'cols'=32] {'rows'}, use_global_device_ids=true, to_apply=%region_13.14 | all-reduce | flops 2048 | bytes 16384 | tf_op jit(solution)/shard_map/pmax | solution.py:63
  482.1 12.7 psum.43
  494.8 51.9 %while.70 = (s32[]{:T(128)}, f32[16,2,256]{2,1,0:T(2,128)S(1)}, f32[2048]{0:T(1024)S(1)}, f32[2048]{0:T(1024)S(1)}, bf16[16,256,128]{2,1,0:T(8,128)(2,1)}, /*ind...) while((s32[]{:T(128)}, f32[16,2,256]{2,1,0:T(2,128)S(1)}, f32[2048]{0:T(1024)S(1)}, ...), condition=%wide.region_19.20_spmd, body=%wide.region_15.19_spmd.sunk | while | flops 139034368 | bytes 4884061 | solution.py:31
  495.8 1.8 fusion.85
  502.3 1.8 fusion.85
  512.0 1.8 fusion.85
  518.5 1.8 fusion.85
  534.7 1.8 fusion.85
  546.8 109.9 %pmax.44 = f32[4096]{0:T(1024)S(1)} all-reduce(f32[4096]{0:T(1024)S(1)} %bitcast.145), channel_id=1, replica_groups=mesh['rows'=8,'cols'=32] {'cols'}, use_global_device_ids=true, to_apply=%region_20.21 | all-reduce | flops 4096 | bytes 32768 | tf_op jit(solution)/shard_map/pmax | solution.py:57
  656.7 110.3 %psum.44 = f32[4096]{0:T(1024)S(1)} all-reduce(f32[4096]{0:T(1024)S(1)} %exponential_multiply_fusion.1), channel_id=1, replica_groups=mesh['rows'=8,'cols'=32] {'cols'}, use_global_device_ids=true, to_apply=%region_21.22 | all-reduce | flops 4096 | bytes 32768 | tf_op jit(solution)/shard_map/psum | solution.py:58
  767.0 49.6 %while.73 = (s32[]{:T(128)}, f32[2048]{0:T(1024)S(1)}, f32[2048]{0:T(1024)S(1)}, f32[16,256]{1,0:T(8,128)S(1)}, f32[16,256]{1,0:T(8,128)S(1)}, /*index=5*/bf16[1...) while((s32[]{:T(128)}, f32[2048]{0:T(1024)S(1)}, ...), condition=%wide.region_26.27_spmd.clone, body=%wide.region_22.26_spmd.clone.sunk | while | flops 139044608 | bytes 4973176 | solution.py:52
  816.6 67.8 %pmax.45 = f32[2048]{0:T(1024)S(1)} all-reduce(f32[2048]{0:T(1024)S(1)} %get-tuple-element.246), channel_id=1, replica_groups=mesh['rows'=8,'cols'=32] {'rows'}, use_global_device_ids=true, to_apply=%region_27.28 | all-reduce | flops 2048 | bytes 16384 | tf_op jit(solution)/shard_map/pmax | solution.py:63
  884.4 12.7 psum.45
  897.2 51.8 %while.71 = (s32[]{:T(128)}, f32[16,2,256]{2,1,0:T(2,128)S(1)}, f32[2048]{0:T(1024)S(1)}, f32[2048]{0:T(1024)S(1)}, bf16[16,256,128]{2,1,0:T(8,128)(2,1)}, /*ind...) while((s32[]{:T(128)}, f32[16,2,256]{2,1,0:T(2,128)S(1)}, f32[2048]{0:T(1024)S(1)}, ...), condition=%wide.region_33.34_spmd, body=%wide.region_29.33_spmd.sunk | while | flops 139034368 | bytes 4884061 | solution.py:31
  949.0 109.9 %pmax.46 = f32[4096]{0:T(1024)S(1)} all-reduce(f32[4096]{0:T(1024)S(1)} %bitcast.147), channel_id=1, replica_groups=mesh['rows'=8,'cols'=32] {'cols'}, use_global_device_ids=true, to_apply=%region_34.35 | all-reduce | flops 4096 | bytes 32768 | tf_op jit(solution)/shard_map/pmax | solution.py:57
  1059.0 110.3 %psum.46 = f32[4096]{0:T(1024)S(1)} all-reduce(f32[4096]{0:T(1024)S(1)} %exponential_multiply_fusion), channel_id=1, replica_groups=mesh['rows'=8,'cols'=32] {'cols'}, use_global_device_ids=true, to_apply=%region_35.36 | all-reduce | flops 4096 | bytes 32768 | tf_op jit(solution)/shard_map/psum | solution.py:58
  1169.9 49.6 %while.74 = (s32[]{:T(128)}, f32[2048]{0:T(1024)S(1)}, f32[2048]{0:T(1024)S(1)}, f32[16,256]{1,0:T(8,128)S(1)}, f32[16,256]{1,0:T(8,128)S(1)}, /*index=5*/bf16[1...) while((s32[]{:T(128)}, f32[2048]{0:T(1024)S(1)}, ...), condition=%wide.region_40.41_spmd.clone, body=%wide.region_36.40_spmd.clone.sunk | while | flops 139044608 | bytes 4973176 | solution.py:52
  1219.5 67.8 %pmax.47 = f32[2048]{0:T(1024)S(1)} all-reduce(f32[2048]{0:T(1024)S(1)} %get-tuple-element.249), channel_id=1, replica_groups=mesh['rows'=8,'cols'=32] {'rows'}, use_global_device_ids=true, to_apply=%region_41.42 | all-reduce | flops 2048 | bytes 16384 | tf_op jit(solution)/shard_map/pmax | solution.py:63
  1287.3 12.7 psum.47
  (558 shorter events, 295.3 us)
Async XLA Ops:
  7.2 79.0 %all-gather.2.cloned.1.call-start = ((), (), s32[]{:S(2)}) async-start(), calls=%async_computation | async-start | bytes 1081344 | tf_op jit(solution)/shard_map/all_gather | solution.py:73
  360.5 134.3 %copy-start.1 = (f32[2048]{0:T(1024)S(1)}, f32[2048]{0:T(1024)}, u32[]{:S(2)}) copy-start(f32[2048]{0:T(1024)} %get-tuple-element.941) | copy-start | bytes 24580
  1169.3 0.6 copy-start
Sparse Core Ops, SparseCore 0:
  10.6 75.5 all-gather.1
where the time goes:
time: 1310 us
  blocking collectives  909 us (69%)
  matrix products  170 us (13%)
  other arithmetic  131 us (10%)
  waiting for transfers between devices  76.8 us (6%)
  between operations  14.3 us (1%)
    pmax x3, blocking collectives, join_cols(): upper = lax.pmax(top, 'cols')  332 us
    psum x3, blocking collectives, join_cols(): whole = lax.psum(total * jnp.exp(top - upper), 'cols')  331 us
    pmax x3, blocking collectives, join_rows(): upper = lax.pmax(top, 'rows')  208 us
    dot_general x96, matrix products, inner_cost(): lax.dot_general(xb, targets, (((1,), (1,)), ((), ())), preferred_element_...  170 us
    reduce_sum x96, other arithmetic, inner_cost(): xnorm = jnp.sum(jnp.square(xb.astype(jnp.float32)), axis=1)  91.7 us
    all_gather x1, waiting for transfers between devices, local(): gathered = lax.all_gather(logged, 'cols', axis=0, tiled=True)  76.1 us
    psum x3, blocking collectives, join_rows(): whole = lax.psum(total * jnp.exp(top - upper), 'rows')  38 us
  transfers between devices with their start and end apart: 1, of which 1 were waited for; matrix products, arithmetic and copies ran while one was open for 0% of the time, Pallas kernels for 0%

commit v1 on v0

v1 whole, which is shorter than its diff:
```python
import functools

import jax
import jax.numpy as jnp
from jax import lax
from jax.experimental import pallas as pl
from jax.experimental.pallas import tpu as pltpu
from jax.sharding import PartitionSpec as P

NX, NZ, NR = 4, 8, 8
F32, BF16 = jnp.float32, jnp.bfloat16
NT = (((1,), (1,)), ((), ()))
TI = 256
TJ = 256
MESH = pl.DeviceIdType.MESH


def dot(a, b, dims=(((1,), (0,)), ((), ()))):
    return lax.dot_general(a, b, dims, preferred_element_type=F32)


def flat(ref, rows, start=0):
    return jnp.concatenate([ref[start + k : start + k + 1, :] for k in range(rows)], axis=1)


def put(ref, value, start=0):
    for k in range(value.shape[1] // 128):
        ref[start + k : start + k + 1, :] = value[:, k * 128 : (k + 1) * 128]


def pieces(value, count):
    out = []
    for k in range(count):
        part = value.astype(BF16).astype(F32)
        out.append(part)
        value = value - part
    return out


def stack_pieces(value, count, rows=16):
    n = value.shape[1]
    index = lax.broadcasted_iota(jnp.int32, (rows, n), 0)
    out = jnp.zeros((rows, n), F32)
    for k, part in enumerate(pieces(value, count)):
        out = jnp.where(index == k, jnp.broadcast_to(part, (rows, n)), out)
    return out.astype(BF16)


def selector(rows, count):
    return (lax.broadcasted_iota(jnp.int32, (rows, 128), 1) < count).astype(F32).astype(BF16)


def square_sums(block):
    wide = block.astype(F32)
    high, low = pieces(wide * wide, 2)
    ones = jnp.ones((8, block.shape[1]), BF16)
    total = dot(ones, high.astype(BF16), NT) + dot(ones, low.astype(BF16), NT)
    return total[0:1, :]


def columns_of(stacked, eye):
    return dot(eye, stacked, NT).astype(BF16)


def kernel(
    x_ref, y_ref, la_ref, lb_ref, g_ref, f_out, g_out,
    xv, ya, p, eye, sel, mt, ct, w, alpha, beta, rowstat, colstat, xn, yn, v1, lse,
    xbuf, zbuf, rbuf,
    gx_send, gx_recv, gz_send, gz_recv, x_send, x_recv, z_send, z_recv, r_send, r_recv,
):
    n, m = xv.shape[0], ya.shape[0]
    nb, mb = n // 128, m // 128
    tiles = n // TI
    row = lax.axis_index("rows")
    col = lax.axis_index("cols")
    px, pz = col // NZ, lax.rem(col, NZ)

    def at_x(k):
        return (row, lax.rem(px + k, NX) * NZ + pz)

    def at_z(k):
        return (row, px * NZ + lax.rem(pz + k, NZ))

    def at_r(k):
        return (lax.rem(row + k, NR), col)

    barrier = pltpu.get_barrier_semaphore()
    for at, count in ((at_x, NX), (at_z, NZ), (at_r, NR)):
        for k in range(1, count):
            pl.semaphore_signal(barrier, inc=1, device_id=at(k), device_id_type=MESH)
    pl.semaphore_wait(barrier, NX + NZ + NR - 3)

    def shard(cx, cz):
        return xv.at[pl.ds(pl.multiple_of((cx * NZ + cz) * 128, 128), 128), pl.ds(0, 128)]

    def remote(src, dst, send, recv, device):
        return pltpu.make_async_remote_copy(
            src_ref=src, dst_ref=dst, send_sem=send, recv_sem=recv, device_id=device, device_id_type=MESH
        )

    def x_copy(k):
        own = shard(px, pz)
        return remote(own, own, gx_send.at[k], gx_recv.at[k], at_x(k))

    def z_copy(cx, cz, way, slot):
        block = shard(cx, cz)
        return remote(block, block, gz_send.at[way, slot], gz_recv.at[way, slot], at_z(1 if way == 0 else NZ - 1))

    def came_x(s):
        return lax.rem(px + NX - s, NX)

    own_rows = pl.ds(pl.multiple_of(col * 128, 128), 128)
    xv[own_rows, 0:128] = x_ref[...]
    for k in range(1, NX):
        x_copy(k).start()
    for way in range(2):
        z_copy(px, pz, way, 0).start()

    index = lax.broadcasted_iota(jnp.int32, (TI, TI), 0) == lax.broadcasted_iota(jnp.int32, (TI, TI), 1)
    eye[...] = jnp.where(index, 1.0, 0.0).astype(BF16)
    sel[...] = selector(TI, 3)
    ya[:, 128:256] = jnp.zeros((m, 128), BF16)
    xv[:, 128:256] = jnp.zeros((n, 128), BF16)
    for k in range(m // TI):
        cut = pl.ds(k * TI, TI)
        block = y_ref[cut, :]
        ya[cut, 0:128] = (block.astype(F32) * 4.0).astype(BF16)
        norm = square_sums(block)
        put(yn, norm, 2 * k)
        u = lb_ref[:, cut] + 2.0 * g_ref[:, cut] - 2.0 * norm
        ya[cut, 128:144] = columns_of(stack_pieces(u, 3), eye[...])

    for s in range(1, NX):
        x_copy(s).wait_recv()
        for way in range(2):
            z_copy(came_x(s), pz, way, s).start()

    def pair(first, second):
        rows_1 = pl.ds(pl.multiple_of(first * 128, 128), 128)
        rows_2 = pl.ds(pl.multiple_of(second * 128, 128), 128)
        points = jnp.concatenate([xv[rows_1, 0:128], xv[rows_2, 0:128]], axis=0)
        points = jnp.concatenate([points, sel[...]], axis=1)
        top = total = None
        for k in range(m // TJ):
            s = dot(ya[k * TJ : (k + 1) * TJ, :], points, NT).reshape(TJ // 8, 8, 256)
            here = jnp.max(s, axis=0)
            if k == 0:
                top = here
                total = jnp.sum(jnp.exp(s - top[None]), axis=0)
            else:
                upper = jnp.maximum(top, here)
                total = total * jnp.exp(top - upper) + jnp.sum(jnp.exp(s - upper[None]), axis=0)
                top = upper
        best = jnp.max(top, axis=0, keepdims=True)
        whole = jnp.sum(total * jnp.exp(top - best), axis=0, keepdims=True)
        for ref, value in ((0, best), (nb, whole)):
            rowstat[pl.ds(ref + first, 1), :] = value[:, 0:128]
            rowstat[pl.ds(ref + second, 1), :] = value[:, 128:256]

    def near(k, carry):
        pair(came_x(2 * k) * NZ + pz, came_x(2 * k + 1) * NZ + pz)
        return carry

    def middle(k, carry):
        hop, s = k // NX + 1, lax.rem(k, NX)
        cx = came_x(s)
        up, down = lax.rem(pz + NZ - hop, NZ), lax.rem(pz + hop, NZ)
        z_copy(cx, up, 0, k).wait_recv()
        z_copy(cx, down, 1, k).wait_recv()

        @pl.when((k < 2 * NX) | ((k >= 2 * NX) & (s < 2)))
        def forward_up():
            z_copy(cx, up, 0, k + NX).start()

        @pl.when(k < 2 * NX)
        def forward_down():
            z_copy(cx, down, 1, k + NX).start()

        @pl.when((k >= 2 * NX) & (s >= 2))
        def forward_last():
            z_copy(cx, down, 1, k + NX - 2).start()

        pair(cx * NZ + up, cx * NZ + down)
        return carry

    def far(k, carry):
        opposite = lax.rem(pz + NZ // 2, NZ)

        @pl.when(k == 0)
        def from_up():
            for s in range(2):
                z_copy(came_x(s), opposite, 0, 3 * NX + s).wait_recv()

        @pl.when(k == 1)
        def from_down():
            for s in range(2):
                z_copy(came_x(s + 2), opposite, 1, 3 * NX + s).wait_recv()

        pair(came_x(2 * k) * NZ + opposite, came_x(2 * k + 1) * NZ + opposite)
        return carry

    lax.fori_loop(0, 2, near, 0)
    lax.fori_loop(0, 3 * NX, middle, 0)
    lax.fori_loop(0, 2, far, 0)

    def spread(buf, send, recv, at, me, count, rows):
        view = pl.ds(0, rows)
        for k in range(1, count):
            own = buf.at[me, view, :]
            remote(own, own, send.at[k], recv.at[k], at(k)).start()

    def collect(buf, send, recv, at, me, count, rows):
        view = pl.ds(0, rows)
        for k in range(1, count):
            own = buf.at[me, view, :]
            remote(own, own, send.at[k], recv.at[k], at(k)).wait()

    def join(buf, count, size):
        tops = [buf[k, 0:size, :] for k in range(count)]
        sums = [buf[k, size : 2 * size, :] for k in range(count)]
        top = functools.reduce(jnp.maximum, tops)
        total = functools.reduce(lambda a, b: a + b, [s * jnp.exp(t - top) for t, s in zip(tops, sums)])
        return top, total

    def add(buf, count, size):
        return functools.reduce(lambda a, b: a + b, [buf[k, 0:size, :] for k in range(count)])

    def over(buf, send, recv, at, me, count, rows, meanwhile=None):
        spread(buf, send, recv, at, me, count, rows)
        if meanwhile is not None:
            meanwhile()
        collect(buf, send, recv, at, me, count, rows)

    def over_x(step, rows, meanwhile=None):
        over(xbuf.at[step], x_send.at[step], x_recv.at[step], at_x, px, NX, rows, meanwhile)

    def over_z(step, rows):
        over(zbuf.at[step], z_send.at[step], z_recv.at[step], at_z, pz, NZ, rows)

    def over_r(step, rows):
        over(rbuf.at[step], r_send.at[step], r_recv.at[step], at_r, row, NR, rows)

    def row_norms():
        def one(k, carry):
            norm = square_sums(xv[pl.ds(pl.multiple_of(k * TI, TI), TI), 0:128])
            xn[pl.ds(2 * k, 1), :] = norm[:, 0:128]
            xn[pl.ds(2 * k + 1, 1), :] = norm[:, 128:256]
            return carry

        lax.fori_loop(0, tiles, one, 0)

    xbuf[0, px] = rowstat[...]
    over_x(0, 2 * nb, row_norms)
    top, total = join(xbuf.at[0], NX, nb)
    zbuf[0, pz, 0:nb, :] = top
    zbuf[0, pz, nb : 2 * nb, :] = total
    over_z(0, 2 * nb)
    top, total = join(zbuf.at[0], NZ, nb)
    v1[...] = la_ref[...] - (top + jnp.log(total))
    alpha[...] = stack_pieces(flat(v1, nb), 3)

    def place(k, carry):
        cut = pl.ds(pl.multiple_of(k * TI, TI), TI)
        xv[cut, 128:144] = columns_of(alpha[:, cut], eye[...])
        return carry

    lax.fori_loop(0, tiles, place, 0)

    def tile(t, carry):
        cut = pl.ds(pl.multiple_of(t * TI, TI), TI)
        points = xv[cut, :]
        for k in range(m // 256):
            lanes = slice(k * 256, (k + 1) * 256)
            weights = jnp.concatenate([ya[lanes, 0:128], sel[...]], axis=1)
            s = dot(points, weights, NT)
            top = jnp.max(s, axis=0, keepdims=True)
            e = jnp.exp(s - top)
            mt[pl.ds(t, 1), lanes] = top
            ct[pl.ds(t, 1), lanes] = jnp.sum(e, axis=0, keepdims=True)
            p[cut, lanes] = e.astype(BF16)
        return carry

    lax.fori_loop(0, tiles, tile, 0)
    top = jnp.max(mt[...], axis=0, keepdims=True)
    total = jnp.sum(ct[...] * jnp.exp(mt[...] - top), axis=0, keepdims=True)
    put(rbuf.at[0, row], top)
    put(rbuf.at[0, row], total, mb)
    over_r(0, 2 * mb)
    top, total = join(rbuf.at[0], NR, mb)
    lse[...] = top + jnp.log(total)
    w[...] = jnp.exp(mt[...] - flat(lse, mb))
    weight_b = jnp.exp(lb_ref[...])

    def row_product(step, scale):
        full = w[...] * scale
        high = full.astype(BF16)
        beta[0:tiles, :] = high
        beta[tiles : 2 * tiles, :] = (full - high.astype(F32)).astype(BF16)

        def one(t, carry):
            cut = pl.ds(pl.multiple_of(t * TI, TI), TI)
            out = dot(beta[...], p[cut, :], NT)
            which = lax.broadcasted_iota(jnp.int32, out.shape, 0)
            mine = jnp.sum(jnp.where((which == t) | (which == t + tiles), out, 0.0), axis=0, keepdims=True)
            xbuf[step, px, pl.ds(2 * t, 1), :] = mine[:, 0:128]
            xbuf[step, px, pl.ds(2 * t + 1, 1), :] = mine[:, 128:256]
            return carry

        lax.fori_loop(0, tiles, one, 0)
        over_x(step, nb)
        zbuf[step, pz, 0:nb, :] = add(xbuf.at[step], NX, nb)
        over_z(step, nb)
        return add(zbuf.at[step], NZ, nb)

    def col_product(step, rowsum):
        rowstat[0:nb, :] = jnp.exp(la_ref[...]) / rowsum
        alpha[...] = stack_pieces(flat(rowstat, nb), 2)

        def one(t, acc):
            cut = pl.ds(pl.multiple_of(t * TI, TI), TI)
            out = dot(alpha[:, cut], p[cut, :])
            return acc + out[0:8, :] * w[pl.ds(t, 1), :]

        acc = lax.fori_loop(0, tiles, one, jnp.zeros((8, m), F32))
        put(rbuf.at[step, row], jnp.sum(acc, axis=0, keepdims=True))
        over_r(step, mb)
        return add(rbuf.at[step], NR, mb)

    rowsum = row_product(1, weight_b)
    colsum = col_product(1, rowsum)
    colstat[...] = colsum
    rowsum = row_product(2, weight_b / flat(colstat, mb))
    f_out[...] = xn[...] + 0.5 * (v1[...] - jnp.log(rowsum))
    colsum = col_product(2, rowsum)
    g_out[...] = yn[...] - 0.5 * (lse[...] + jnp.log(colsum))

    for k in range(1, NX):
        x_copy(k).wait_send()
    for slot in range(3 * NX + 2):
        for way in range(2):
            z_copy(px, pz, way, slot).wait_send()


def local(logged, targets, log_a, log_b, start_g):
    n, m = log_a.shape[0], log_b.shape[0]
    nb, mb = n // 128, m // 128
    tiles = n // TI
    dma = pltpu.SemaphoreType.DMA
    vmem = pl.BlockSpec(memory_space=pltpu.VMEM)
    f, g = pl.pallas_call(
        kernel,
        out_shape=(jax.ShapeDtypeStruct((nb, 128), F32), jax.ShapeDtypeStruct((mb, 128), F32)),
        in_specs=[vmem] * 5,
        out_specs=(vmem, vmem),
        scratch_shapes=[
            pltpu.VMEM((n, 256), BF16),
            pltpu.VMEM((m, 256), BF16),
            pltpu.VMEM((n, m), BF16),
            pltpu.VMEM((TI, TI), BF16),
            pltpu.VMEM((TI, 128), BF16),
            pltpu.VMEM((tiles, m), F32),
            pltpu.VMEM((tiles, m), F32),
            pltpu.VMEM((tiles, m), F32),
            pltpu.VMEM((16, n), BF16),
            pltpu.VMEM((2 * tiles, m), BF16),
            pltpu.VMEM((2 * nb, 128), F32),
            pltpu.VMEM((mb, 128), F32),
            pltpu.VMEM((nb, 128), F32),
            pltpu.VMEM((mb, 128), F32),
            pltpu.VMEM((nb, 128), F32),
            pltpu.VMEM((mb, 128), F32),
            pltpu.VMEM((3, NX, 2 * nb, 128), F32),
            pltpu.VMEM((3, NZ, 2 * nb, 128), F32),
            pltpu.VMEM((3, NR, 2 * mb, 128), F32),
            dma((NX,)),
            dma((NX,)),
            dma((2, 3 * NX + 2)),
            dma((2, 3 * NX + 2)),
            dma((3, NX)),
            dma((3, NX)),
            dma((3, NZ)),
            dma((3, NZ)),
            dma((3, NR)),
            dma((3, NR)),
        ],
        compiler_params=pltpu.CompilerParams(
            collective_id=0, has_side_effects=True, vmem_limit_bytes=50 * 1024 * 1024
        ),
    )(logged, targets, log_a.reshape(nb, 128), log_b.reshape(1, m), start_g.reshape(1, m))
    return f.reshape(n), g.reshape(m)


def solution(mesh):
    placed = (P(("rows", "cols"), None), P("cols", None), P("rows"), P("cols"), P("cols"))
    return jax.shard_map(
        local, mesh=mesh, in_specs=placed, out_specs=(P("rows"), P("cols")), check_vma=False
    )
```

time: 1310 us -> 115 us (0.09)
  blocking collectives: 909 us -> 0 us
  matrix products: 170 us -> 0 us
  other arithmetic: 131 us -> 0 us
  Pallas kernels: 0 us -> 109 us
  waiting for transfers between devices: 76.8 us -> 0 us
  between operations: 14.3 us -> 0.65 us
    pmax x6 -> x0, blocking collectives: 540 us -> none  [the longest x3 332 us: join_cols(): upper = lax.pmax(top, 'cols')]
    psum x6 -> x0, blocking collectives: 369 us -> none  [the longest x3 331 us: join_cols(): whole = lax.psum(total * jnp.exp(top - upper), 'cols')]
    dot_general x96 -> x0, matrix products: 170 us -> none  [inner_cost(): lax.dot_general(xb, targets, (((1,), (1,)), ((), ())), preferred_element_...]
    reduce_sum x193 -> x0, other arithmetic: 129 us -> none  [the longest x96 91.7 us: inner_cost(): xnorm = jnp.sum(jnp.square(xb.astype(jnp.float32)), axis=1)]
    pallas_call x0 -> x1, Pallas kernels: none -> 109 us  [local(): pl.pallas_call(kernel, out_shape=(jax.ShapeDtypeStruct((nb, 128), F32), j...]
    all_gather x1 -> x0, waiting for transfers between devices: 76.1 us -> none  [local(): gathered = lax.all_gather(logged, 'cols', axis=0, tiled=True)]
  transfers between devices with their start and end apart: 1 -> 0, of which waited for: 1 -> 0; matrix products, arithmetic and copies ran while one was open for 0% -> 0% of each run, Pallas kernels for 0% -> 0%
where the time goes in v1:
time: 115 us
  Pallas kernels  109 us (95%)
  local copies, waits for them, and re-layouts  5.11 us (4%)
    pallas_call x1, Pallas kernels, local(): pl.pallas_call(kernel, out_shape=(jax.ShapeDtypeStruct((nb, 128), F32), j...  109 us
    unnamed x12, local copies, waits for them, and re-layouts  5.11 us

profile of v1, /device:TPU:1, one launch (start us, length us, event | category | flops | bytes accessed | tf_op | source)
XLA Modules:
  0.0 115.2 jit_solution(18442052045942379355)
XLA Ops:
  0.6 0.0 copy-start
  0.6 1.0 copy-done
  1.7 0.0 copy-start.1
  1.7 0.8 copy-done.1
  2.4 0.0 copy-start.2
  2.4 0.7 copy-done.2
  3.1 0.0 copy-start.3
  3.2 0.7 copy-done.3
  3.8 0.0 copy-start.4
  3.8 0.7 copy-done.4
  4.5 109.4 %shard_map.68 = (f32[32,128]{1,0:T(8,128)S(1)}, f32[16,128]{1,0:T(8,128)S(1)}) custom-call(bf16[128,128]{1,0:T(8,128)(2,1)S(1)} %copy-done.1, bf16[2048,128]{1,0:T(8,128)(2,1)S(1)} %copy-done, f32[32,128]{1,0:T(8,128)S(1)} %bitcast.5, f32[1,2048]{1,0:T(1,128)S(1)} %bitcast.7, f32[1,2048]{1,0:T(1,128)S(1)} %bitcast.8), custom_call_target="tpu_custom_call" | custom-call | tf_op jit(solution)/shard_map/pallas_call | solution.py:350
  114.0 0.6 copy.9
  114.6 0.6 copy.10
Async XLA Ops:
  0.6 1.0 copy-start
  1.7 0.8 copy-start.1
  2.4 0.7 copy-start.2
  3.1 0.7 copy-start.3
  3.8 0.7 copy-start.4

commit v2 on v1

v2 whole, which is shorter than its diff:
```python
import functools

import jax
import jax.numpy as jnp
from jax import lax
from jax.experimental import pallas as pl
from jax.experimental.pallas import tpu as pltpu
from jax.sharding import PartitionSpec as P

NX, NZ, NR = 4, 8, 8
F32, BF16 = jnp.float32, jnp.bfloat16
NT = (((1,), (1,)), ((), ()))
TI = 256
TJ = 256
WIDE = 1024
MESH = pl.DeviceIdType.MESH


def dot(a, b, dims=(((1,), (0,)), ((), ()))):
    return lax.dot_general(a, b, dims, preferred_element_type=F32)


def flat(ref, rows, start=0):
    return jnp.concatenate([ref[start + k : start + k + 1, :] for k in range(rows)], axis=1)


def put(ref, value, start=0):
    for k in range(value.shape[1] // 128):
        ref[start + k : start + k + 1, :] = value[:, k * 128 : (k + 1) * 128]


def pieces(value, count):
    out = []
    for k in range(count):
        part = value.astype(BF16).astype(F32)
        out.append(part)
        value = value - part
    return out


def stack_pieces(value, count, rows=16):
    n = value.shape[1]
    index = lax.broadcasted_iota(jnp.int32, (rows, n), 0)
    out = jnp.zeros((rows, n), F32)
    for k, part in enumerate(pieces(value, count)):
        out = jnp.where(index == k, jnp.broadcast_to(part, (rows, n)), out)
    return out.astype(BF16)


def selector(rows, count):
    return (lax.broadcasted_iota(jnp.int32, (rows, 128), 1) < count).astype(F32).astype(BF16)


def square_sums(block):
    wide = block.astype(F32)
    high, low = pieces(wide * wide, 2)
    ones = jnp.ones((8, block.shape[1]), BF16)
    total = dot(ones, high.astype(BF16), NT) + dot(ones, low.astype(BF16), NT)
    return total[0:1, :]


def columns_of(stacked, eye):
    return dot(eye, stacked, NT).astype(BF16)


def kernel(
    x_hbm, y_hbm, la_hbm, lb_hbm, g_hbm, f_out, g_out,
    y_ref, la_ref, lb_ref, g_ref,
    xv, ya, p, eye, sel, mt, ct, w, alpha, beta, rowstat, colstat, xn, yn, v1, lse,
    xpair, zpair, rpair, xbuf, zbuf, rbuf, local_sem,
    gx_send, gx_recv, gz_send, gz_recv, x_send, x_recv, z_send, z_recv, r_send, r_recv,
):
    n, m = xv.shape[0], ya.shape[0]
    nb, mb = n // 128, m // 128
    tiles = n // TI
    row = lax.axis_index("rows")
    col = lax.axis_index("cols")
    px, pz = col // NZ, lax.rem(col, NZ)

    def at_x(k):
        return (row, lax.rem(px + k, NX) * NZ + pz)

    def at_z(k):
        return (row, px * NZ + lax.rem(pz + k, NZ))

    def at_r(k):
        return (lax.rem(row + k, NR), col)

    barrier = pltpu.get_barrier_semaphore()
    for at, count in ((at_x, NX), (at_z, NZ), (at_r, NR)):
        for k in range(1, count):
            pl.semaphore_signal(barrier, inc=1, device_id=at(k), device_id_type=MESH)

    own_rows = pl.ds(pl.multiple_of(col * 128, 128), 128)
    moves = (
        (x_hbm, xv.at[own_rows, pl.ds(0, 128)]), (y_hbm, y_ref), (la_hbm, la_ref), (lb_hbm, lb_ref), (g_hbm, g_ref),
    )
    fetch = [pltpu.make_async_copy(src, dst, local_sem.at[k]) for k, (src, dst) in enumerate(moves)]
    for one in fetch:
        one.start()
    index = lax.broadcasted_iota(jnp.int32, (TI, TI), 0) == lax.broadcasted_iota(jnp.int32, (TI, TI), 1)
    eye[...] = jnp.where(index, 1.0, 0.0).astype(BF16)
    sel[...] = selector(sel.shape[0], 3)
    ya[:, 128:256] = jnp.zeros((m, 128), BF16)
    xv[:, 128:256] = jnp.zeros((n, 128), BF16)
    fetch[0].wait()
    pl.semaphore_wait(barrier, NX + NZ + NR - 3)

    def remote(src, dst, send, recv, device):
        return pltpu.make_async_remote_copy(
            src_ref=src, dst_ref=dst, send_sem=send, recv_sem=recv, device_id=device, device_id_type=MESH
        )

    def came_x(s):
        return lax.rem(px + NX - s, NX)

    def came_z(k):
        return lax.rem(pz + NZ - k, NZ)

    def shard_rows(cx, cz):
        return pl.ds(pl.multiple_of((cx * NZ + cz) * 128, 128), 128)

    def shard(cx, cz):
        return xv.at[shard_rows(cx, cz), pl.ds(0, 128)]

    def z_copy(k):
        own = shard(px, pz)
        return remote(own, own, gz_send.at[k], gz_recv.at[k], at_z(k))

    def x_copy(k, s):
        block = shard(px, came_z(k))
        return remote(block, block, gx_send.at[k, s], gx_recv.at[k, s], at_x(s))

    def turn(q):
        odd = lax.rem(q, 2)
        return odd * ((q + 1) // 2) + (1 - odd) * lax.rem(NZ - q // 2, NZ)

    for s in range(1, NX):
        x_copy(0, s).start()
    for q in range(1, NZ):
        z_copy((q + 1) // 2 if q % 2 else NZ - q // 2).start()
    for one in fetch[1:]:
        one.wait()

    for k in range(m // TI):
        cut = pl.ds(k * TI, TI)
        block = y_ref[cut, :]
        ya[cut, 0:128] = (block.astype(F32) * 4.0).astype(BF16)
        norm = square_sums(block)
        put(yn, norm, 2 * k)
        u = lb_ref[:, cut] + 2.0 * g_ref[:, cut] - 2.0 * norm
        ya[cut, 128:144] = columns_of(stack_pieces(u, 3), eye[...])

    def forward(q):
        k = turn(q)
        z_copy(k).wait_recv()
        for s in range(1, NX):
            x_copy(k, s).start()

    def pass_1(q, carry):
        @pl.when(q < NZ - 2)
        def ahead():
            forward(q + 2)

        k = turn(q)
        for s in range(1, NX):
            remote(shard(came_x(s), came_z(k)), shard(came_x(s), came_z(k)), gx_send.at[k, s], gx_recv.at[k, s],
                   at_x(s)).wait_recv()
        points = jnp.concatenate([xv[shard_rows(came_x(s), came_z(k)), 0:128] for s in range(NX)], axis=0)
        points = jnp.concatenate([points, sel[0 : NX * 128, :]], axis=1)
        top = total = None
        for j in range(m // TJ):
            s = dot(ya[j * TJ : (j + 1) * TJ, :], points, NT).reshape(TJ // 8, 8, NX * 128)
            here = jnp.max(s, axis=0)
            if j == 0:
                top = here
                total = jnp.sum(jnp.exp(s - top[None]), axis=0)
            else:
                upper = jnp.maximum(top, here)
                total = total * jnp.exp(top - upper) + jnp.sum(jnp.exp(s - upper[None]), axis=0)
                top = upper
        best = jnp.max(top, axis=0, keepdims=True)
        whole = jnp.sum(total * jnp.exp(top - best), axis=0, keepdims=True)
        for start, value in ((0, best), (nb, whole)):
            for s in range(NX):
                rowstat[pl.ds(start + came_x(s) * NZ + came_z(k), 1), :] = value[:, s * 128 : (s + 1) * 128]
        return carry

    forward(1)
    lax.fori_loop(0, NZ, pass_1, 0)

    def spread(buf, send, recv, at, me, count, rows):
        view = pl.ds(0, rows)
        for k in range(1, count):
            own = buf.at[me, view, :]
            remote(own, own, send.at[k], recv.at[k], at(k)).start()

    def collect(buf, send, recv, at, me, count, rows):
        view = pl.ds(0, rows)
        for k in range(1, count):
            own = buf.at[me, view, :]
            remote(own, own, send.at[k], recv.at[k], at(k)).wait()

    def join(buf, count, size):
        tops = [buf[k, 0:size, :].astype(F32) for k in range(count)]
        sums = [buf[k, size : 2 * size, :].astype(F32) for k in range(count)]
        top = functools.reduce(jnp.maximum, tops)
        total = functools.reduce(lambda a, b: a + b, [s * jnp.exp(t - top) for t, s in zip(tops, sums)])
        return top, total

    def add(buf, count, size):
        return functools.reduce(lambda a, b: a + b, [buf[k, 0:size, :].astype(F32) for k in range(count)])

    def pack(ref, top, total):
        size = top.shape[0]
        near = top.astype(BF16)
        ref[0:size, :] = near
        ref[size : 2 * size, :] = (total * jnp.exp(top - near.astype(F32))).astype(BF16)

    def over(buf, send, recv, at, me, count, rows, meanwhile=None):
        spread(buf, send, recv, at, me, count, rows)
        if meanwhile is not None:
            meanwhile()
        collect(buf, send, recv, at, me, count, rows)

    def over_x(buf, step, meanwhile=None):
        over(buf, x_send.at[step], x_recv.at[step], at_x, px, NX, buf.shape[1], meanwhile)

    def over_z(buf, step):
        over(buf, z_send.at[step], z_recv.at[step], at_z, pz, NZ, buf.shape[1])

    def over_r(buf, step):
        over(buf, r_send.at[step], r_recv.at[step], at_r, row, NR, buf.shape[1])

    def row_norms():
        def one(k, carry):
            norm = square_sums(xv[pl.ds(pl.multiple_of(k * TI, TI), TI), 0:128])
            xn[pl.ds(2 * k, 1), :] = norm[:, 0:128]
            xn[pl.ds(2 * k + 1, 1), :] = norm[:, 128:256]
            return carry

        lax.fori_loop(0, tiles, one, 0)

    pack(xpair.at[px], rowstat[0:nb, :], rowstat[nb : 2 * nb, :])
    over_x(xpair, 0, row_norms)
    pack(zpair.at[pz], *join(xpair, NX, nb))
    over_z(zpair, 0)
    top, total = join(zpair, NZ, nb)
    v1[...] = la_ref[...] - (top + jnp.log(total))
    alpha[...] = stack_pieces(flat(v1, nb), 3)

    def place(k, carry):
        cut = pl.ds(pl.multiple_of(k * TI, TI), TI)
        xv[cut, 128:144] = columns_of(alpha[:, cut], eye[...])
        return carry

    lax.fori_loop(0, tiles, place, 0)

    def tile(t, carry):
        cut = pl.ds(pl.multiple_of(t * TI, TI), TI)
        points = xv[cut, :]
        for k in range(m // WIDE):
            lanes = slice(k * WIDE, (k + 1) * WIDE)
            weights = jnp.concatenate([ya[lanes, 0:128], sel[...]], axis=1)
            s = dot(points, weights, NT)
            top = jnp.max(s, axis=0, keepdims=True)
            e = jnp.exp(s - top)
            mt[pl.ds(t, 1), lanes] = top
            ct[pl.ds(t, 1), lanes] = jnp.sum(e, axis=0, keepdims=True)
            p[cut, lanes] = e.astype(BF16)
        return carry

    lax.fori_loop(0, tiles, tile, 0, unroll=2)
    top = jnp.max(mt[...], axis=0, keepdims=True)
    total = jnp.sum(ct[...] * jnp.exp(mt[...] - top), axis=0, keepdims=True)
    put(colstat, top)
    put(colstat, total, mb)
    pack(rpair.at[row], colstat[0:mb, :], colstat[mb : 2 * mb, :])
    over_r(rpair, 0)
    top, total = join(rpair, NR, mb)
    lse[...] = top + jnp.log(total)
    w[...] = jnp.exp(mt[...] - flat(lse, mb))
    weight_b = jnp.exp(lb_ref[...])

    def row_product(step, scale):
        full = w[...] * scale
        high = full.astype(BF16)
        beta[0:tiles, :] = high
        beta[tiles : 2 * tiles, :] = (full - high.astype(F32)).astype(BF16)

        for half in range(2):
            cut = pl.ds(half * (n // 2), n // 2)
            out = dot(beta[...], p[cut, :], NT)
            which = lax.broadcasted_iota(jnp.int32, out.shape, 0)
            own = lax.broadcasted_iota(jnp.int32, out.shape, 1) // TI + half * (tiles // 2)
            mine = jnp.sum(jnp.where((which == own) | (which == own + tiles), out, 0.0), axis=0, keepdims=True)
            put(rowstat, mine, half * (nb // 2))
        xbuf[step - 1, px] = rowstat[0:nb, :].astype(BF16)
        over_x(xbuf.at[step - 1], step)
        zbuf[step - 1, pz] = add(xbuf.at[step - 1], NX, nb).astype(BF16)
        over_z(zbuf.at[step - 1], step)
        return add(zbuf.at[step - 1], NZ, nb)

    def col_product(step, rowsum):
        rowstat[0:nb, :] = jnp.exp(la_ref[...]) / rowsum
        alpha[...] = stack_pieces(flat(rowstat, nb), 2)

        def one(t, acc):
            cut = pl.ds(pl.multiple_of(t * TI, TI), TI)
            out = dot(alpha[:, cut], p[cut, :])
            return acc + out[0:8, :] * w[pl.ds(t, 1), :]

        acc = lax.fori_loop(0, tiles, one, jnp.zeros((8, m), F32), unroll=16)
        put(rbuf.at[step - 1, row], jnp.sum(acc, axis=0, keepdims=True))
        over_r(rbuf.at[step - 1], step)
        return add(rbuf.at[step - 1], NR, mb)

    rowsum = row_product(1, weight_b)
    colsum = col_product(1, rowsum)
    colstat[0:mb, :] = colsum
    rowsum = row_product(2, weight_b / flat(colstat, mb))
    f_out[...] = xn[...] + 0.5 * (v1[...] - jnp.log(rowsum))
    colsum = col_product(2, rowsum)
    g_out[...] = yn[...] - 0.5 * (lse[...] + jnp.log(colsum))

    for k in range(NZ):
        if k:
            z_copy(k).wait_send()
        for s in range(1, NX):
            x_copy(k, s).wait_send()


def local(logged, targets, log_a, log_b, start_g):
    n, m = log_a.shape[0], log_b.shape[0]
    nb, mb = n // 128, m // 128
    tiles = n // TI
    dma = pltpu.SemaphoreType.DMA
    vmem = pl.BlockSpec(memory_space=pltpu.VMEM)
    anywhere = pl.BlockSpec(memory_space=pl.ANY)
    f, g = pl.pallas_call(
        kernel,
        out_shape=(jax.ShapeDtypeStruct((nb, 128), F32), jax.ShapeDtypeStruct((mb, 128), F32)),
        in_specs=[anywhere] * 5,
        out_specs=(vmem, vmem),
        scratch_shapes=[
            pltpu.VMEM((m, 128), BF16),
            pltpu.VMEM((nb, 128), F32),
            pltpu.VMEM((1, m), F32),
            pltpu.VMEM((1, m), F32),
            pltpu.VMEM((n, 256), BF16),
            pltpu.VMEM((m, 256), BF16),
            pltpu.VMEM((n, m), BF16),
            pltpu.VMEM((TI, TI), BF16),
            pltpu.VMEM((WIDE, 128), BF16),
            pltpu.VMEM((tiles, m), F32),
            pltpu.VMEM((tiles, m), F32),
            pltpu.VMEM((tiles, m), F32),
            pltpu.VMEM((16, n), BF16),
            pltpu.VMEM((2 * tiles, m), BF16),
            pltpu.VMEM((2 * nb, 128), F32),
            pltpu.VMEM((2 * mb, 128), F32),
            pltpu.VMEM((nb, 128), F32),
            pltpu.VMEM((mb, 128), F32),
            pltpu.VMEM((nb, 128), F32),
            pltpu.VMEM((mb, 128), F32),
            pltpu.VMEM((NX, 2 * nb, 128), BF16),
            pltpu.VMEM((NZ, 2 * nb, 128), BF16),
            pltpu.VMEM((NR, 2 * mb, 128), BF16),
            pltpu.VMEM((2, NX, nb, 128), BF16),
            pltpu.VMEM((2, NZ, nb, 128), BF16),
            pltpu.VMEM((2, NR, mb, 128), F32),
            dma((5,)),
            dma((NZ, NX)),
            dma((NZ, NX)),
            dma((NZ,)),
            dma((NZ,)),
            dma((3, NX)),
            dma((3, NX)),
            dma((3, NZ)),
            dma((3, NZ)),
            dma((3, NR)),
            dma((3, NR)),
        ],
        compiler_params=pltpu.CompilerParams(
            collective_id=0, has_side_effects=True, vmem_limit_bytes=50 * 1024 * 1024
        ),
    )(logged, targets, log_a.reshape(nb, 128), log_b.reshape(1, m), start_g.reshape(1, m))
    return f.reshape(n), g.reshape(m)


def solution(mesh):
    placed = (P(("rows", "cols"), None), P("cols", None), P("rows"), P("cols"), P("cols"))
    return jax.shard_map(
        local, mesh=mesh, in_specs=placed, out_specs=(P("rows"), P("cols")), check_vma=False
    )
```

time: 115 us -> 105 us (0.913)
  Pallas kernels: 109 us -> 99.4 us
    pallas_call x1, Pallas kernels: 109 us -> 99.4 us  [local(): pl.pallas_call(kernel, out_shape=(jax.ShapeDtypeStruct((nb, 128), F32), j...]
where the time goes in v2:
time: 105 us
  Pallas kernels  99.4 us (95%)
  local copies, waits for them, and re-layouts  5.11 us (5%)
    pallas_call x1, Pallas kernels, local(): pl.pallas_call(kernel, out_shape=(jax.ShapeDtypeStruct((nb, 128), F32), j...  99.4 us
    unnamed x12, local copies, waits for them, and re-layouts  5.11 us

profile of v2, /device:TPU:1, one launch (start us, length us, event | category | flops | bytes accessed | tf_op | source)
XLA Modules:
  0.0 105.1 jit_solution(8037318192775530338)
XLA Ops:
  0.6 0.0 copy-start
  0.6 1.0 copy-done
  1.7 0.0 copy-start.1
  1.7 0.8 copy-done.1
  2.4 0.0 copy-start.2
  2.4 0.7 copy-done.2
  3.1 0.0 copy-start.3
  3.2 0.7 copy-done.3
  3.8 0.0 copy-start.4
  3.8 0.7 copy-done.4
  4.5 99.4 %shard_map.68 = (f32[32,128]{1,0:T(8,128)S(1)}, f32[16,128]{1,0:T(8,128)S(1)}) custom-call(bf16[128,128]{1,0:T(8,128)(2,1)S(1)} %copy-done.1, bf16[2048,128]{1,0:T(8,128)(2,1)S(1)} %copy-done, f32[32,128]{1,0:T(8,128)S(1)} %bitcast.5, f32[1,2048]{1,0:T(1,128)S(1)} %bitcast.7, f32[1,2048]{1,0:T(1,128)S(1)} %bitcast.8), custom_call_target="tpu_custom_call" | custom-call | tf_op jit(solution)/shard_map/pallas_call | solution.py:340
  103.9 0.6 copy.9
  104.5 0.6 copy.10
Async XLA Ops:
  0.6 1.0 copy-start
  1.7 0.8 copy-start.1
  2.4 0.7 copy-start.2
  3.1 0.7 copy-start.3
  3.8 0.7 copy-start.4

commit v3 on v2

v3 whole, which is shorter than its diff:
```python
import functools

import jax
import jax.numpy as jnp
from jax import lax
from jax.experimental import pallas as pl
from jax.experimental.pallas import tpu as pltpu
from jax.sharding import PartitionSpec as P

NX, NZ, NR = 4, 8, 8
F32, BF16 = jnp.float32, jnp.bfloat16
BENT = (1, 7, 2, 6)
NT = (((1,), (1,)), ((), ()))
TI = 256
TJ = 256
WIDE = 512
MESH = pl.DeviceIdType.MESH


def dot(a, b, dims=(((1,), (0,)), ((), ()))):
    return lax.dot_general(a, b, dims, preferred_element_type=F32)


def flat(ref, rows, start=0):
    return jnp.concatenate([ref[start + k : start + k + 1, :] for k in range(rows)], axis=1)


def put(ref, value, start=0):
    for k in range(value.shape[1] // 128):
        ref[start + k : start + k + 1, :] = value[:, k * 128 : (k + 1) * 128]


def pieces(value, count):
    out = []
    for k in range(count):
        part = value.astype(BF16).astype(F32)
        out.append(part)
        value = value - part
    return out


def stack_pieces(value, count, rows=16):
    n = value.shape[1]
    index = lax.broadcasted_iota(jnp.int32, (rows, n), 0)
    out = jnp.zeros((rows, n), F32)
    for k, part in enumerate(pieces(value, count)):
        out = jnp.where(index == k, jnp.broadcast_to(part, (rows, n)), out)
    return out.astype(BF16)


def selector(rows, count):
    return (lax.broadcasted_iota(jnp.int32, (rows, 128), 1) < count).astype(F32).astype(BF16)


def square_sums(block):
    wide = block.astype(F32)
    high, low = pieces(wide * wide, 2)
    ones = jnp.ones((8, block.shape[1]), BF16)
    total = dot(ones, high.astype(BF16), NT) + dot(ones, low.astype(BF16), NT)
    return total[0:1, :]


def columns_of(stacked, eye):
    return dot(eye, stacked, NT).astype(BF16)


def kernel(
    x_hbm, y_hbm, la_hbm, lb_hbm, g_hbm, f_out, g_out,
    y_ref, la_ref, lb_ref, g_ref,
    xv, ya, p, held, eye, sel, best_col, sum_col, w, alpha, rowpart, colpart, rowstat, colstat, xn, yn, v1, lse,
    xpair, zpair, rpair, xbuf, zbuf, rbuf, local_sem,
    gx_send, gx_recv, gz_send, gz_recv, x_send, x_recv, z_send, z_recv, r_send, r_recv,
):
    n, m = xv.shape[0], ya.shape[0]
    nb, mb = n // 128, m // 128
    tiles = n // TI
    row = lax.axis_index("rows")
    col = lax.axis_index("cols")
    px, pz = col // NZ, lax.rem(col, NZ)

    def at_x(k):
        return (row, lax.rem(px + k, NX) * NZ + pz)

    def at_z(k):
        return (row, px * NZ + lax.rem(pz + k, NZ))

    def at_r(k):
        return (lax.rem(row + k, NR), col)

    barrier = pltpu.get_barrier_semaphore()
    for at, count in ((at_x, NX), (at_z, NZ), (at_r, NR)):
        for k in range(1, count):
            pl.semaphore_signal(barrier, inc=1, device_id=at(k), device_id_type=MESH)

    own_rows = pl.ds(pl.multiple_of(col * 128, 128), 128)
    moves = (
        (x_hbm, xv.at[own_rows, pl.ds(0, 128)]), (y_hbm, y_ref), (la_hbm, la_ref), (lb_hbm, lb_ref), (g_hbm, g_ref),
    )
    fetch = [pltpu.make_async_copy(src, dst, local_sem.at[k]) for k, (src, dst) in enumerate(moves)]
    for one in fetch:
        one.start()
    index = lax.broadcasted_iota(jnp.int32, (TI, TI), 0) == lax.broadcasted_iota(jnp.int32, (TI, TI), 1)
    eye[...] = jnp.where(index, 1.0, 0.0).astype(BF16)
    sel[...] = selector(sel.shape[0], 3)
    ya[:, 128:256] = jnp.zeros((m, 128), BF16)
    xv[:, 128:256] = jnp.zeros((n, 128), BF16)
    for one in fetch:
        one.wait()

    for k in range(m // TI):
        cut = pl.ds(k * TI, TI)
        block = y_ref[cut, :]
        ya[cut, 0:128] = (block.astype(F32) * 4.0).astype(BF16)
        norm = square_sums(block)
        put(yn, norm, 2 * k)
        u = lb_ref[:, cut] + 2.0 * g_ref[:, cut] - 2.0 * norm
        ya[cut, 128:144] = columns_of(stack_pieces(u, 3), eye[...])

    pl.semaphore_wait(barrier, NX + NZ + NR - 3)

    def remote(src, dst, send, recv, device):
        return pltpu.make_async_remote_copy(
            src_ref=src, dst_ref=dst, send_sem=send, recv_sem=recv, device_id=device, device_id_type=MESH
        )

    def came_x(s):
        return lax.rem(px + NX - s, NX)

    def came_z(k):
        return lax.rem(pz + NZ - k, NZ)

    def shard_rows(cx, cz):
        return pl.ds(pl.multiple_of((cx * NZ + cz) * 128, 128), 128)

    def shard(cx, cz):
        return xv.at[shard_rows(cx, cz), pl.ds(0, 128)]

    def z_copy(k):
        own = shard(px, pz)
        return remote(own, own, gz_send.at[k], gz_recv.at[k], at_z(k))

    def x_copy(k, s):
        block = shard(px, came_z(k))
        return remote(block, block, gx_send.at[k, s], gx_recv.at[k, s], at_x(s))

    def turn(q):
        odd = lax.rem(q, 2)
        return odd * ((q + 1) // 2) + (1 - odd) * lax.rem(NZ - q // 2, NZ)

    for s in range(1, NX):
        x_copy(0, s).start()
    for q in range(1, NZ):
        z_copy((q + 1) // 2 if q % 2 else NZ - q // 2).start()
    def bent_copy(k):
        block = shard(came_x(2), pz)
        return remote(block, block, gx_send.at[k, 2], gx_recv.at[k, 2], at_z(k))

    def forward(q):
        k = turn(q)
        z_copy(k).wait_recv()
        x_copy(k, 1).start()
        x_copy(k, 3).start()

        @pl.when(q > len(BENT))
        def opposite():
            x_copy(k, 2).start()

    def pass_1(q, carry):
        @pl.when(q < NZ - 2)
        def ahead():
            forward(q + 2)

        k = turn(q)
        for s in range(1, NX):
            remote(shard(came_x(s), came_z(k)), shard(came_x(s), came_z(k)), gx_send.at[k, s], gx_recv.at[k, s],
                   at_x(s)).wait_recv()

        @pl.when(q == 0)
        def bent():
            for distance in BENT:
                bent_copy(distance).start()

        points = jnp.concatenate([xv[shard_rows(came_x(s), came_z(k)), 0:128] for s in range(NX)], axis=0)
        points = jnp.concatenate([points, sel[0 : NX * 128, :]], axis=1)
        top = total = None
        for j in range(m // TJ):
            s = dot(ya[j * TJ : (j + 1) * TJ, :], points, NT).reshape(TJ // 8, 8, NX * 128)
            here = jnp.max(s, axis=0)
            if j == 0:
                top = here
                total = jnp.sum(jnp.exp(s - top[None]), axis=0)
            else:
                upper = jnp.maximum(top, here)
                total = total * jnp.exp(top - upper) + jnp.sum(jnp.exp(s - upper[None]), axis=0)
                top = upper
        best = jnp.max(top, axis=0, keepdims=True)
        whole = jnp.sum(total * jnp.exp(top - best), axis=0, keepdims=True)
        for start, value in ((0, best), (nb, whole)):
            for s in range(NX):
                rowstat[pl.ds(start + came_x(s) * NZ + came_z(k), 1), :] = value[:, s * 128 : (s + 1) * 128]
        return carry

    forward(1)
    lax.fori_loop(0, NZ, pass_1, 0)

    def spread(buf, send, recv, at, me, count):
        for k in range(1, count):
            remote(buf.at[me], buf.at[me], send.at[k], recv.at[k], at(k)).start()

    def collect(buf, send, recv, at, me, count):
        for k in range(1, count):
            remote(buf.at[me], buf.at[me], send.at[k], recv.at[k], at(k)).wait()

    def on_x(buf, slot):
        return (buf, x_send.at[slot], x_recv.at[slot], at_x, px, NX)

    def on_z(buf, slot):
        return (buf, z_send.at[slot], z_recv.at[slot], at_z, pz, NZ)

    def on_r(buf, slot):
        return (buf, r_send.at[slot], r_recv.at[slot], at_r, row, NR)

    def join(buf, count, size):
        tops = [buf[k, 0:size, :].astype(F32) for k in range(count)]
        sums = [buf[k, size : 2 * size, :].astype(F32) for k in range(count)]
        top = functools.reduce(jnp.maximum, tops)
        total = functools.reduce(lambda a, b: a + b, [s * jnp.exp(t - top) for t, s in zip(tops, sums)])
        return top, total

    def add(buf, count, size):
        return functools.reduce(lambda a, b: a + b, [buf[k, 0:size, :].astype(F32) for k in range(count)])

    def pack(ref, top, total):
        size = top.shape[0]
        near = top.astype(BF16)
        ref[0:size, :] = near
        ref[size : 2 * size, :] = (total * jnp.exp(top - near.astype(F32))).astype(BF16)

    def row_norms():
        def one(k, carry):
            norm = square_sums(xv[pl.ds(pl.multiple_of(k * TI, TI), TI), 0:128])
            xn[pl.ds(2 * k, 1), :] = norm[:, 0:128]
            xn[pl.ds(2 * k + 1, 1), :] = norm[:, 128:256]
            return carry

        lax.fori_loop(0, tiles, one, 0)

    pack(xpair.at[px], rowstat[0:nb, :], rowstat[nb : 2 * nb, :])
    spread(*on_x(xpair, 0))
    row_norms()
    collect(*on_x(xpair, 0))
    pack(zpair.at[pz], *join(xpair, NX, nb))
    spread(*on_z(zpair, 0))
    collect(*on_z(zpair, 0))
    top, total = join(zpair, NZ, nb)
    v1[...] = la_ref[...] - (top + jnp.log(total))
    alpha[...] = stack_pieces(flat(v1, nb), 3)

    def place(k, carry):
        cut = pl.ds(pl.multiple_of(k * TI, TI), TI)
        xv[cut, 128:144] = columns_of(alpha[:, cut], eye[...])
        return carry

    lax.fori_loop(0, tiles, place, 0)

    halves = range(2)
    nh, mh = n // 2, m // 2

    def block(q, carry):
        lanes = pl.ds(pl.multiple_of(q * WIDE, WIDE), WIDE)
        weights = jnp.concatenate([ya[lanes, 0:128], sel[...]], axis=1)
        top = None
        for t in range(tiles):
            s = dot(xv[t * TI : (t + 1) * TI, :], weights, NT)
            held[t * TI : (t + 1) * TI, :] = s
            here = jnp.max(s.reshape(TI // 8, 8, WIDE), axis=0)
            top = here if top is None else jnp.maximum(top, here)
        top = jnp.max(top, axis=0, keepdims=True)
        total = jnp.zeros((8, WIDE), F32)
        for t in range(tiles):
            e = jnp.exp(held[t * TI : (t + 1) * TI, :].reshape(TI // 8, 8, WIDE) - top[None])
            total = total + jnp.sum(e, axis=0)
            p[t * TI : (t + 1) * TI, lanes] = e.reshape(TI, WIDE).astype(BF16)
        best_col[:, lanes] = top
        sum_col[:, lanes] = jnp.sum(total, axis=0, keepdims=True)
        return carry

    for c in halves:
        lax.fori_loop(c * (mh // WIDE), (c + 1) * (mh // WIDE), block, 0)
        put(rpair.at[c, row], best_col[:, c * mh : (c + 1) * mh])
        put(rpair.at[c, row], sum_col[:, c * mh : (c + 1) * mh], mb // 2)
        spread(*on_r(rpair.at[c], c))

    def col_half(c):
        return slice(c * mh, (c + 1) * mh), slice(c * (mb // 2), (c + 1) * (mb // 2))

    def row_half(h):
        return slice(h * nh, (h + 1) * nh), slice(h * (nb // 2), (h + 1) * (nb // 2))

    def scale_of(step, c):
        lanes, rows = col_half(c)
        if step == 1:
            collect(*on_r(rpair.at[c], c))
            top, total = join(rpair.at[c], NR, mb // 2)
            lse[rows, :] = top + jnp.log(total)
            w[:, lanes] = jnp.exp(best_col[:, lanes] - flat(lse, mb // 2, c * (mb // 2)))
            return jnp.exp(lb_ref[:, lanes]) * w[:, lanes]
        collect(*on_r(rbuf.at[0, c], 2 + c))
        colstat[rows, :] = add(rbuf.at[0, c], NR, mb // 2)
        return jnp.exp(lb_ref[:, lanes]) * w[:, lanes] / flat(colstat, mb // 2, c * (mb // 2))

    for step in (1, 2):
        for c in halves:
            lanes = col_half(c)[0]
            beta = stack_pieces(scale_of(step, c), 2)
            if c == 0:
                rowpart[...] = dot(beta, p[:, lanes], NT)[0:8, :]
            else:
                for h in halves:
                    cut, rows = row_half(h)
                    out = rowpart[:, cut] + dot(beta, p[cut, lanes], NT)[0:8, :]
                    put(rowstat, jnp.sum(out, axis=0, keepdims=True), h * (nb // 2))
                    xbuf[step - 1, h, px] = rowstat[rows, :].astype(BF16)
                    spread(*on_x(xbuf.at[step - 1, h], 2 * step + h))
        for h in halves:
            collect(*on_x(xbuf.at[step - 1, h], 2 * step + h))
            zbuf[step - 1, h, pz] = add(xbuf.at[step - 1, h], NX, nb // 2).astype(BF16)
            spread(*on_z(zbuf.at[step - 1, h], 2 * step + h))
        for h in halves:
            cut, rows = row_half(h)
            collect(*on_z(zbuf.at[step - 1, h], 2 * step + h))
            rowsum = add(zbuf.at[step - 1, h], NZ, nb // 2)
            rowstat[rows, :] = jnp.exp(la_ref[rows, :]) / rowsum
            if step == 2:
                f_out[rows, :] = xn[rows, :] + 0.5 * (v1[rows, :] - jnp.log(rowsum))
            share = stack_pieces(flat(rowstat, nb // 2, h * (nb // 2)), 2)
            if h == 0:
                colpart[...] = dot(share, p[cut, :])[0:8, :]
            else:
                for c in halves:
                    lanes = col_half(c)[0]
                    out = colpart[:, lanes] + dot(share, p[cut, lanes])[0:8, :]
                    put(rbuf.at[step - 1, c, row], jnp.sum(out, axis=0, keepdims=True) * w[:, lanes])
                    spread(*on_r(rbuf.at[step - 1, c], 2 * step + c))
    for c in halves:
        rows = col_half(c)[1]
        collect(*on_r(rbuf.at[1, c], 4 + c))
        g_out[rows, :] = yn[rows, :] - 0.5 * (lse[rows, :] + jnp.log(add(rbuf.at[1, c], NR, mb // 2)))

    for k in range(NZ):
        if k:
            z_copy(k).wait_send()
        for s in range(1, NX):
            (bent_copy(k) if s == 2 and k in BENT else x_copy(k, s)).wait_send()


def local(logged, targets, log_a, log_b, start_g):
    n, m = log_a.shape[0], log_b.shape[0]
    nb, mb = n // 128, m // 128
    tiles = n // TI
    dma = pltpu.SemaphoreType.DMA
    vmem = pl.BlockSpec(memory_space=pltpu.VMEM)
    anywhere = pl.BlockSpec(memory_space=pltpu.HBM)
    f, g = pl.pallas_call(
        kernel,
        out_shape=(jax.ShapeDtypeStruct((nb, 128), F32), jax.ShapeDtypeStruct((mb, 128), F32)),
        in_specs=[anywhere] * 5,
        out_specs=(vmem, vmem),
        scratch_shapes=[
            pltpu.VMEM((m, 128), BF16),
            pltpu.VMEM((nb, 128), F32),
            pltpu.VMEM((1, m), F32),
            pltpu.VMEM((1, m), F32),
            pltpu.VMEM((n, 256), BF16),
            pltpu.VMEM((m, 256), BF16),
            pltpu.VMEM((n, m), BF16),
            pltpu.VMEM((n, WIDE), F32),
            pltpu.VMEM((TI, TI), BF16),
            pltpu.VMEM((WIDE, 128), BF16),
            pltpu.VMEM((1, m), F32),
            pltpu.VMEM((1, m), F32),
            pltpu.VMEM((1, m), F32),
            pltpu.VMEM((16, n), BF16),
            pltpu.VMEM((8, n), F32),
            pltpu.VMEM((8, m), F32),
            pltpu.VMEM((2 * nb, 128), F32),
            pltpu.VMEM((mb, 128), F32),
            pltpu.VMEM((nb, 128), F32),
            pltpu.VMEM((mb, 128), F32),
            pltpu.VMEM((nb, 128), F32),
            pltpu.VMEM((mb, 128), F32),
            pltpu.VMEM((NX, 2 * nb, 128), BF16),
            pltpu.VMEM((NZ, 2 * nb, 128), BF16),
            pltpu.VMEM((2, NR, mb, 128), F32),
            pltpu.VMEM((2, 2, NX, nb // 2, 128), BF16),
            pltpu.VMEM((2, 2, NZ, nb // 2, 128), BF16),
            pltpu.VMEM((2, 2, NR, mb // 2, 128), F32),
            dma((5,)),
            dma((NZ, NX)),
            dma((NZ, NX)),
            dma((NZ,)),
            dma((NZ,)),
            dma((6, NX)),
            dma((6, NX)),
            dma((6, NZ)),
            dma((6, NZ)),
            dma((6, NR)),
            dma((6, NR)),
        ],
        compiler_params=pltpu.CompilerParams(
            collective_id=0, has_side_effects=True, vmem_limit_bytes=64 * 1024 * 1024
        ),
    )(logged, targets, log_a.reshape(nb, 128), log_b.reshape(1, m), start_g.reshape(1, m))
    return f.reshape(n), g.reshape(m)


def solution(mesh):
    placed = (P(("rows", "cols"), None), P("cols", None), P("rows"), P("cols"), P("cols"))
    return jax.shard_map(
        local, mesh=mesh, in_specs=placed, out_specs=(P("rows"), P("cols")), check_vma=False
    )
```

time: 105 us -> 97.8 us (0.931)
  Pallas kernels: 99.4 us -> 95.1 us
  local copies, waits for them, and re-layouts: 5.11 us -> 1.93 us
    pallas_call x1, Pallas kernels: 99.4 us -> 95.1 us  [local(): pl.pallas_call(kernel, out_shape=(jax.ShapeDtypeStruct((nb, 128), F32), j...]
    unnamed x12 -> x4, local copies, waits for them, and re-layouts: 5.11 us -> 1.93 us
where the time goes in v3:
time: 97.8 us; the launch traced here: 97.7 us
  Pallas kernels  95.1 us (97%)
  local copies, waits for them, and re-layouts  1.93 us (2%)
    pallas_call x1, Pallas kernels, local(): pl.pallas_call(kernel, out_shape=(jax.ShapeDtypeStruct((nb, 128), F32), j...  95.1 us

profile of v3, /device:TPU:1, one launch (start us, length us, event | category | flops | bytes accessed | tf_op | source)
XLA Modules:
  0.0 97.7 jit_solution(7515989559213714840)
XLA Ops:
  0.6 95.1 %shard_map.68 = (f32[32,128]{1,0:T(8,128)}, f32[16,128]{1,0:T(8,128)}) custom-call(bf16[128,128]{1,0:T(8,128)(2,1)} %x_hbm.1, bf16[2048,128]{1,0:T(8,128)(2,1)} %y_hbm.1, f32[32,128]{1,0:T(8,128)} %bitcast.5, f32[1,2048]{1,0:T(1,128)} %bitcast.7, f32[1,2048]{1,0:T(1,128)} %bitcast.8), custom_call_target="tpu_custom_call" | custom-call | tf_op jit(solution)/shard_map/pallas_call | solution.py:364
  95.7 0.0 copy-start
  95.8 1.3 %copy.9 = f32[4096]{0:T(1024)} copy(f32[4096]{0:T(1024)} %bitcast.6) | data formatting | bytes 32768
  97.1 0.0 copy-done
  97.1 0.6 copy.10
Async XLA Ops:
  95.7 1.3 %copy-start = (f32[16,128]{1,0:T(8,128)S(1)}, f32[16,128]{1,0:T(8,128)}, u32[]{:S(2)}) copy-start(f32[16,128]{1,0:T(8,128)} %get-tuple-element.5) | copy-start | bytes 24580

commit v4 on v3

--- a/solution.py
+++ b/solution.py
@@ -14,6 +14,7 @@
 TI = 256
 TJ = 256
 WIDE = 512
+QUARTERS = 4
 MESH = pl.DeviceIdType.MESH
 
 
@@ -65,7 +66,7 @@
 
 
 def kernel(
-    x_hbm, y_hbm, la_hbm, lb_hbm, g_hbm, f_out, g_out,
+    x_hbm, y_hbm, la_hbm, lb_hbm, g_hbm, out,
     y_ref, la_ref, lb_ref, g_ref,
     xv, ya, p, held, eye, sel, best_col, sum_col, w, alpha, rowpart, colpart, rowstat, colstat, xn, yn, v1, lse,
     xpair, zpair, rpair, xbuf, zbuf, rbuf, local_sem,
@@ -104,7 +105,43 @@
     sel[...] = selector(sel.shape[0], 3)
     ya[:, 128:256] = jnp.zeros((m, 128), BF16)
     xv[:, 128:256] = jnp.zeros((n, 128), BF16)
-    for one in fetch:
+    fetch[0].wait()
+    pl.semaphore_wait(barrier, NX + NZ + NR - 3)
+
+    def remote(src, dst, send, recv, device):
+        return pltpu.make_async_remote_copy(
+            src_ref=src, dst_ref=dst, send_sem=send, recv_sem=recv, device_id=device, device_id_type=MESH
+        )
+
+    def came_x(s):
+        return lax.rem(px + NX - s, NX)
+
+    def came_z(k):
+        return lax.rem(pz + NZ - k, NZ)
+
+    def shard_rows(cx, cz):
+        return pl.ds(pl.multiple_of((cx * NZ + cz) * 128, 128), 128)
+
+    def shard(cx, cz):
+        return xv.at[shard_rows(cx, cz), pl.ds(0, 128)]
+
+    def z_copy(k):
+        own = shard(px, pz)
+        return remote(own, own, gz_send.at[k], gz_recv.at[k], at_z(k))
+
+    def x_copy(k, s):
+        block = shard(px, came_z(k))
+        return remote(block, block, gx_send.at[k, s], gx_recv.at[k, s], at_x(s))
+
+    def turn(q):
+        odd = lax.rem(q, 2)
+        return odd * ((q + 1) // 2) + (1 - odd) * lax.rem(NZ - q // 2, NZ)
+
+    for s in range(1, NX):
+        x_copy(0, s).start()
+    for q in range(1, NZ):
+        z_copy((q + 1) // 2 if q % 2 else NZ - q // 2).start()
+    for one in fetch[1:]:
         one.wait()
 
     for k in range(m // TI):
@@ -116,41 +153,6 @@
         u = lb_ref[:, cut] + 2.0 * g_ref[:, cut] - 2.0 * norm
         ya[cut, 128:144] = columns_of(stack_pieces(u, 3), eye[...])
 
-    pl.semaphore_wait(barrier, NX + NZ + NR - 3)
-
-    def remote(src, dst, send, recv, device):
-        return pltpu.make_async_remote_copy(
-            src_ref=src, dst_ref=dst, send_sem=send, recv_sem=recv, device_id=device, device_id_type=MESH
-        )
-
-    def came_x(s):
-        return lax.rem(px + NX - s, NX)
-
-    def came_z(k):
-        return lax.rem(pz + NZ - k, NZ)
-
-    def shard_rows(cx, cz):
-        return pl.ds(pl.multiple_of((cx * NZ + cz) * 128, 128), 128)
-
-    def shard(cx, cz):
-        return xv.at[shard_rows(cx, cz), pl.ds(0, 128)]
-
-    def z_copy(k):
-        own = shard(px, pz)
-        return remote(own, own, gz_send.at[k], gz_recv.at[k], at_z(k))
-
-    def x_copy(k, s):
-        block = shard(px, came_z(k))
-        return remote(block, block, gx_send.at[k, s], gx_recv.at[k, s], at_x(s))
-
-    def turn(q):
-        odd = lax.rem(q, 2)
-        return odd * ((q + 1) // 2) + (1 - odd) * lax.rem(NZ - q // 2, NZ)
-
-    for s in range(1, NX):
-        x_copy(0, s).start()
-    for q in range(1, NZ):
-        z_copy((q + 1) // 2 if q % 2 else NZ - q // 2).start()
     def bent_copy(k):
         block = shard(came_x(2), pz)
         return remote(block, block, gx_send.at[k, 2], gx_recv.at[k, 2], at_z(k))
@@ -261,7 +263,7 @@
         xv[cut, 128:144] = columns_of(alpha[:, cut], eye[...])
         return carry
 
-    lax.fori_loop(0, tiles, place, 0)
+    lax.fori_loop(0, tiles, place, 0, unroll=8)
 
     halves = range(2)
     nh, mh = n // 2, m // 2
@@ -285,41 +287,47 @@
         sum_col[:, lanes] = jnp.sum(total, axis=0, keepdims=True)
         return carry
 
-    for c in halves:
-        lax.fori_loop(c * (mh // WIDE), (c + 1) * (mh // WIDE), block, 0)
-        put(rpair.at[c, row], best_col[:, c * mh : (c + 1) * mh])
-        put(rpair.at[c, row], sum_col[:, c * mh : (c + 1) * mh], mb // 2)
+    def columns(c, count):
+        lanes, rows = m // count, mb // count
+        return slice(c * lanes, (c + 1) * lanes), slice(c * rows, (c + 1) * rows), rows
+
+    for c in range(QUARTERS):
+        lanes, _, size = columns(c, QUARTERS)
+        lax.fori_loop(c * (m // QUARTERS // WIDE), (c + 1) * (m // QUARTERS // WIDE), block, 0)
+        put(rpair.at[c, row], best_col[:, lanes])
+        put(rpair.at[c, row], sum_col[:, lanes], size)
         spread(*on_r(rpair.at[c], c))
-
-    def col_half(c):
-        return slice(c * mh, (c + 1) * mh), slice(c * (mb // 2), (c + 1) * (mb // 2))
 
     def row_half(h):
         return slice(h * nh, (h + 1) * nh), slice(h * (nb // 2), (h + 1) * (nb // 2))
 
     def scale_of(step, c):
-        lanes, rows = col_half(c)
+        count = QUARTERS if step == 1 else 2
+        lanes, rows, size = columns(c, count)
         if step == 1:
             collect(*on_r(rpair.at[c], c))
-            top, total = join(rpair.at[c], NR, mb // 2)
+            top, total = join(rpair.at[c], NR, size)
             lse[rows, :] = top + jnp.log(total)
-            w[:, lanes] = jnp.exp(best_col[:, lanes] - flat(lse, mb // 2, c * (mb // 2)))
+            w[:, lanes] = jnp.exp(best_col[:, lanes] - flat(lse, size, c * size))
             return jnp.exp(lb_ref[:, lanes]) * w[:, lanes]
-        collect(*on_r(rbuf.at[0, c], 2 + c))
-        colstat[rows, :] = add(rbuf.at[0, c], NR, mb // 2)
-        return jnp.exp(lb_ref[:, lanes]) * w[:, lanes] / flat(colstat, mb // 2, c * (mb // 2))
+        collect(*on_r(rbuf.at[0, c], QUARTERS + c))
+        colstat[rows, :] = add(rbuf.at[0, c], NR, size)
+        return jnp.exp(lb_ref[:, lanes]) * w[:, lanes] / flat(colstat, size, c * size)
 
     for step in (1, 2):
-        for c in halves:
-            lanes = col_half(c)[0]
+        count = QUARTERS if step == 1 else 2
+        for c in range(count):
+            lanes = columns(c, count)[0]
             beta = stack_pieces(scale_of(step, c), 2)
             if c == 0:
                 rowpart[...] = dot(beta, p[:, lanes], NT)[0:8, :]
+            elif c < count - 1:
+                rowpart[...] = rowpart[...] + dot(beta, p[:, lanes], NT)[0:8, :]
             else:
                 for h in halves:
                     cut, rows = row_half(h)
-                    out = rowpart[:, cut] + dot(beta, p[cut, lanes], NT)[0:8, :]
-                    put(rowstat, jnp.sum(out, axis=0, keepdims=True), h * (nb // 2))
+                    both = rowpart[:, cut] + dot(beta, p[cut, lanes], NT)[0:8, :]
+                    put(rowstat, jnp.sum(both, axis=0, keepdims=True), h * (nb // 2))
                     xbuf[step - 1, h, px] = rowstat[rows, :].astype(BF16)
                     spread(*on_x(xbuf.at[step - 1, h], 2 * step + h))
         for h in halves:
@@ -332,20 +340,20 @@
             rowsum = add(zbuf.at[step - 1, h], NZ, nb // 2)
             rowstat[rows, :] = jnp.exp(la_ref[rows, :]) / rowsum
             if step == 2:
-                f_out[rows, :] = xn[rows, :] + 0.5 * (v1[rows, :] - jnp.log(rowsum))
+                out[rows, :] = xn[rows, :] + 0.5 * (v1[rows, :] - jnp.log(rowsum))
             share = stack_pieces(flat(rowstat, nb // 2, h * (nb // 2)), 2)
             if h == 0:
                 colpart[...] = dot(share, p[cut, :])[0:8, :]
             else:
                 for c in halves:
-                    lanes = col_half(c)[0]
-                    out = colpart[:, lanes] + dot(share, p[cut, lanes])[0:8, :]
-                    put(rbuf.at[step - 1, c, row], jnp.sum(out, axis=0, keepdims=True) * w[:, lanes])
-                    spread(*on_r(rbuf.at[step - 1, c], 2 * step + c))
+                    lanes = columns(c, 2)[0]
+                    both = colpart[:, lanes] + dot(share, p[cut, lanes])[0:8, :]
+                    put(rbuf.at[step - 1, c, row], jnp.sum(both, axis=0, keepdims=True) * w[:, lanes])
+                    spread(*on_r(rbuf.at[step - 1, c], QUARTERS + 2 * (step - 1) + c))
     for c in halves:
-        rows = col_half(c)[1]
-        collect(*on_r(rbuf.at[1, c], 4 + c))
-        g_out[rows, :] = yn[rows, :] - 0.5 * (lse[rows, :] + jnp.log(add(rbuf.at[1, c], NR, mb // 2)))
+        rows = columns(c, 2)[1]
+        collect(*on_r(rbuf.at[1, c], QUARTERS + 2 + c))
+        out[nb + c * (mb // 2) : nb + (c + 1) * (mb // 2), :] = yn[rows, :] - 0.5 * (lse[rows, :] + jnp.log(add(rbuf.at[1, c], NR, mb // 2)))
 
     for k in range(NZ):
         if k:
@@ -361,11 +369,11 @@
     dma = pltpu.SemaphoreType.DMA
     vmem = pl.BlockSpec(memory_space=pltpu.VMEM)
     anywhere = pl.BlockSpec(memory_space=pltpu.HBM)
-    f, g = pl.pallas_call(
+    out = pl.pallas_call(
         kernel,
-        out_shape=(jax.ShapeDtypeStruct((nb, 128), F32), jax.ShapeDtypeStruct((mb, 128), F32)),
+        out_shape=jax.ShapeDtypeStruct((nb + mb, 128), F32),
         in_specs=[anywhere] * 5,
-        out_specs=(vmem, vmem),
+        out_specs=vmem,
         scratch_shapes=[
             pltpu.VMEM((m, 128), BF16),
             pltpu.VMEM((nb, 128), F32),
@@ -391,7 +399,7 @@
             pltpu.VMEM((mb, 128), F32),
             pltpu.VMEM((NX, 2 * nb, 128), BF16),
             pltpu.VMEM((NZ, 2 * nb, 128), BF16),
-            pltpu.VMEM((2, NR, mb, 128), F32),
+            pltpu.VMEM((QUARTERS, NR, 2 * mb // QUARTERS, 128), F32),
             pltpu.VMEM((2, 2, NX, nb // 2, 128), BF16),
             pltpu.VMEM((2, 2, NZ, nb // 2, 128), BF16),
             pltpu.VMEM((2, 2, NR, mb // 2, 128), F32),
@@ -404,14 +412,14 @@
             dma((6, NX)),
             dma((6, NZ)),
             dma((6, NZ)),
-            dma((6, NR)),
-            dma((6, NR)),
+            dma((QUARTERS + 4, NR)),
+            dma((QUARTERS + 4, NR)),
         ],
         compiler_params=pltpu.CompilerParams(
             collective_id=0, has_side_effects=True, vmem_limit_bytes=64 * 1024 * 1024
         ),
     )(logged, targets, log_a.reshape(nb, 128), log_b.reshape(1, m), start_g.reshape(1, m))
-    return f.reshape(n), g.reshape(m)
+    return out[:nb].reshape(n), out[nb:].reshape(m)
 
 
 def solution(mesh):

time: 97.8 us -> 95.3 us (0.974)
  Pallas kernels: 95.1 us -> 91.8 us
    pallas_call x1, Pallas kernels: 95.1 us -> 91.8 us  [local(): pl.pallas_call(kernel, out_shape=jax.ShapeDtypeStruct((nb + mb, 128), F32...]
    reshape x0 -> x2, local copies, waits for them, and re-layouts: none -> 2.62 us  [local(): return (out[:nb].reshape(n), out[nb:].reshape(m))]
    unnamed x4 -> x0, local copies, waits for them, and re-layouts: 1.93 us -> none
where the time goes in v4:
time: 95.3 us; the launch traced here: 95.1 us
  Pallas kernels  91.8 us (96%)
  local copies, waits for them, and re-layouts  2.62 us (3%)
    pallas_call x1, Pallas kernels, local(): pl.pallas_call(kernel, out_shape=jax.ShapeDtypeStruct((nb + mb, 128), F32...  91.8 us
    reshape x2, local copies, waits for them, and re-layouts, local(): return (out[:nb].reshape(n), out[nb:].reshape(m))  2.62 us

profile of v4, /device:TPU:1, one launch (start us, length us, event | category | flops | bytes accessed | tf_op | source)
XLA Modules:
  0.0 95.1 jit_solution(13996662979860407464)
XLA Ops:
  0.6 91.8 %shard_map.68 = f32[48,128]{1,0:T(8,128)} custom-call(bf16[128,128]{1,0:T(8,128)(2,1)} %x_hbm.1, bf16[2048,128]{1,0:T(8,128)(2,1)} %y_hbm.1, f32[32,128]{1,0:T(8,128)} %bitcast.7, f32[1,2048]{1,0:T(1,128)} %bitcast.8, f32[1,2048]{1,0:T(1,128)} %bitcast.9), custom_call_target="tpu_custom_call" | custom-call | tf_op jit(solution)/shard_map/pallas_call | solution.py:372
  92.4 1.3 %slice_bitcast_fusion.1 = f32[2048]{0:T(1024)} fusion(f32[48,128]{1,0:T(8,128)} %shard_map.68), kind=kLoop, calls=%fused_computation.1 | loop fusion | bytes 16384 | tf_op jit(solution)/shard_map/reshape | solution.py:422
  93.7 1.3 %slice_bitcast_fusion = f32[4096]{0:T(1024)} fusion(f32[48,128]{1,0:T(8,128)} %shard_map.68), kind=kLoop, calls=%fused_computation | loop fusion | bytes 32768 | tf_op jit(solution)/shard_map/reshape | solution.py:422

commit v5 on v4

--- a/solution.py
+++ b/solution.py
@@ -9,7 +9,7 @@
 
 NX, NZ, NR = 4, 8, 8
 F32, BF16 = jnp.float32, jnp.bfloat16
-BENT = (1, 7, 2, 6)
+AHEAD = 4
 NT = (((1,), (1,)), ((), ()))
 TI = 256
 TJ = 256
@@ -66,7 +66,7 @@
 
 
 def kernel(
-    x_hbm, y_hbm, la_hbm, lb_hbm, g_hbm, out,
+    x_hbm, y_hbm, la_hbm, lb_hbm, g_hbm, f_out, g_out,
     y_ref, la_ref, lb_ref, g_ref,
     xv, ya, p, held, eye, sel, best_col, sum_col, w, alpha, rowpart, colpart, rowstat, colstat, xn, yn, v1, lse,
     xpair, zpair, rpair, xbuf, zbuf, rbuf, local_sem,
@@ -137,7 +137,7 @@
         odd = lax.rem(q, 2)
         return odd * ((q + 1) // 2) + (1 - odd) * lax.rem(NZ - q // 2, NZ)
 
-    for s in range(1, NX):
+    for s in (1, 3, 2):
         x_copy(0, s).start()
     for q in range(1, NZ):
         z_copy((q + 1) // 2 if q % 2 else NZ - q // 2).start()
@@ -153,34 +153,21 @@
         u = lb_ref[:, cut] + 2.0 * g_ref[:, cut] - 2.0 * norm
         ya[cut, 128:144] = columns_of(stack_pieces(u, 3), eye[...])
 
-    def bent_copy(k):
-        block = shard(came_x(2), pz)
-        return remote(block, block, gx_send.at[k, 2], gx_recv.at[k, 2], at_z(k))
-
     def forward(q):
         k = turn(q)
         z_copy(k).wait_recv()
-        x_copy(k, 1).start()
-        x_copy(k, 3).start()
-
-        @pl.when(q > len(BENT))
-        def opposite():
-            x_copy(k, 2).start()
+        for s in (1, 3, 2):
+            x_copy(k, s).start()
 
     def pass_1(q, carry):
-        @pl.when(q < NZ - 2)
+        @pl.when(q < NZ - AHEAD)
         def ahead():
-            forward(q + 2)
+            forward(q + AHEAD)
 
         k = turn(q)
         for s in range(1, NX):
             remote(shard(came_x(s), came_z(k)), shard(came_x(s), came_z(k)), gx_send.at[k, s], gx_recv.at[k, s],
                    at_x(s)).wait_recv()
-
-        @pl.when(q == 0)
-        def bent():
-            for distance in BENT:
-                bent_copy(distance).start()
 
         points = jnp.concatenate([xv[shard_rows(came_x(s), came_z(k)), 0:128] for s in range(NX)], axis=0)
         points = jnp.concatenate([points, sel[0 : NX * 128, :]], axis=1)
@@ -202,7 +189,8 @@
                 rowstat[pl.ds(start + came_x(s) * NZ + came_z(k), 1), :] = value[:, s * 128 : (s + 1) * 128]
         return carry
 
-    forward(1)
+    for q in range(1, AHEAD):
+        forward(q)
     lax.fori_loop(0, NZ, pass_1, 0)
 
     def spread(buf, send, recv, at, me, count):
@@ -340,7 +328,7 @@
             rowsum = add(zbuf.at[step - 1, h], NZ, nb // 2)
             rowstat[rows, :] = jnp.exp(la_ref[rows, :]) / rowsum
             if step == 2:
-                out[rows, :] = xn[rows, :] + 0.5 * (v1[rows, :] - jnp.log(rowsum))
+                f_out[rows, :] = xn[rows, :] + 0.5 * (v1[rows, :] - jnp.log(rowsum))
             share = stack_pieces(flat(rowstat, nb // 2, h * (nb // 2)), 2)
             if h == 0:
                 colpart[...] = dot(share, p[cut, :])[0:8, :]
@@ -353,13 +341,13 @@
     for c in halves:
         rows = columns(c, 2)[1]
         collect(*on_r(rbuf.at[1, c], QUARTERS + 2 + c))
-        out[nb + c * (mb // 2) : nb + (c + 1) * (mb // 2), :] = yn[rows, :] - 0.5 * (lse[rows, :] + jnp.log(add(rbuf.at[1, c], NR, mb // 2)))
+        g_out[rows, :] = yn[rows, :] - 0.5 * (lse[rows, :] + jnp.log(add(rbuf.at[1, c], NR, mb // 2)))
 
     for k in range(NZ):
         if k:
             z_copy(k).wait_send()
         for s in range(1, NX):
-            (bent_copy(k) if s == 2 and k in BENT else x_copy(k, s)).wait_send()
+            x_copy(k, s).wait_send()
 
 
 def local(logged, targets, log_a, log_b, start_g):
@@ -369,11 +357,11 @@
     dma = pltpu.SemaphoreType.DMA
     vmem = pl.BlockSpec(memory_space=pltpu.VMEM)
     anywhere = pl.BlockSpec(memory_space=pltpu.HBM)
-    out = pl.pallas_call(
+    f, g = pl.pallas_call(
         kernel,
-        out_shape=jax.ShapeDtypeStruct((nb + mb, 128), F32),
+        out_shape=(jax.ShapeDtypeStruct((nb, 128), F32), jax.ShapeDtypeStruct((mb, 128), F32)),
         in_specs=[anywhere] * 5,
-        out_specs=vmem,
+        out_specs=(vmem, vmem),
         scratch_shapes=[
             pltpu.VMEM((m, 128), BF16),
             pltpu.VMEM((nb, 128), F32),
@@ -419,7 +407,7 @@
             collective_id=0, has_side_effects=True, vmem_limit_bytes=64 * 1024 * 1024
         ),
     )(logged, targets, log_a.reshape(nb, 128), log_b.reshape(1, m), start_g.reshape(1, m))
-    return out[:nb].reshape(n), out[nb:].reshape(m)
+    return f.reshape(n), g.reshape(m)
 
 
 def solution(mesh):

time: 95.3 us -> 91.8 us (0.963)
  Pallas kernels: 91.8 us -> 89.1 us
    pallas_call x1, Pallas kernels: 91.8 us -> 89.1 us  [local(): pl.pallas_call(kernel, out_shape=(jax.ShapeDtypeStruct((nb, 128), F32), j...]
    reshape x2 -> x0, local copies, waits for them, and re-layouts: 2.62 us -> none  [local(): return (out[:nb].reshape(n), out[nb:].reshape(m))]
    unnamed x0 -> x4, local copies, waits for them, and re-layouts: none -> 1.93 us
where the time goes in v5:
time: 91.8 us; the launch traced here: 91.6 us
  Pallas kernels  89.1 us (97%)
  local copies, waits for them, and re-layouts  1.93 us (2%)
    pallas_call x1, Pallas kernels, local(): pl.pallas_call(kernel, out_shape=(jax.ShapeDtypeStruct((nb, 128), F32), j...  89.1 us
    unnamed x4, local copies, waits for them, and re-layouts  1.93 us

profile of v5, /device:TPU:1, one launch (start us, length us, event | category | flops | bytes accessed | tf_op | source)
XLA Modules:
  0.0 91.6 jit_solution(702838983658424984)
XLA Ops:
  0.6 89.1 %shard_map.68 = (f32[32,128]{1,0:T(8,128)}, f32[16,128]{1,0:T(8,128)}) custom-call(bf16[128,128]{1,0:T(8,128)(2,1)} %x_hbm.1, bf16[2048,128]{1,0:T(8,128)(2,1)} %y_hbm.1, f32[32,128]{1,0:T(8,128)} %bitcast.5, f32[1,2048]{1,0:T(1,128)} %bitcast.7, f32[1,2048]{1,0:T(1,128)} %bitcast.8), custom_call_target="tpu_custom_call" | custom-call | tf_op jit(solution)/shard_map/pallas_call | solution.py:360
  89.7 0.0 copy-start
  89.7 1.3 %copy.9 = f32[4096]{0:T(1024)} copy(f32[4096]{0:T(1024)} %bitcast.6) | data formatting | bytes 32768
  91.0 0.0 copy-done
  91.0 0.6 copy.10
Async XLA Ops:
  89.7 1.3 %copy-start = (f32[16,128]{1,0:T(8,128)S(1)}, f32[16,128]{1,0:T(8,128)}, u32[]{:S(2)}) copy-start(f32[16,128]{1,0:T(8,128)} %get-tuple-element.5) | copy-start | bytes 24580

commit v6 on v5

--- a/solution.py
+++ b/solution.py
@@ -127,11 +127,14 @@
 
     def z_copy(k):
         own = shard(px, pz)
-        return remote(own, own, gz_send.at[k], gz_recv.at[k], at_z(k))
+        return remote(own, own, gz_send, gz_recv.at[k], at_z(k))
 
     def x_copy(k, s):
         block = shard(px, came_z(k))
-        return remote(block, block, gx_send.at[k, s], gx_recv.at[k, s], at_x(s))
+        return remote(block, block, gx_send, gx_recv.at[k], at_x(s))
+
+    def shards(count):
+        return xv.at[pl.ds(0, count * 128), pl.ds(0, 128)]
 
     def turn(q):
         odd = lax.rem(q, 2)
@@ -165,10 +168,7 @@
             forward(q + AHEAD)
 
         k = turn(q)
-        for s in range(1, NX):
-            remote(shard(came_x(s), came_z(k)), shard(came_x(s), came_z(k)), gx_send.at[k, s], gx_recv.at[k, s],
-                   at_x(s)).wait_recv()
-
+        remote(shards(NX - 1), shards(NX - 1), gx_send, gx_recv.at[k], at_x(1)).wait_recv()
         points = jnp.concatenate([xv[shard_rows(came_x(s), came_z(k)), 0:128] for s in range(NX)], axis=0)
         points = jnp.concatenate([points, sel[0 : NX * 128, :]], axis=1)
         top = total = None
@@ -195,11 +195,11 @@
 
     def spread(buf, send, recv, at, me, count):
         for k in range(1, count):
-            remote(buf.at[me], buf.at[me], send.at[k], recv.at[k], at(k)).start()
+            remote(buf.at[me], buf.at[me], send, recv, at(k)).start()
 
     def collect(buf, send, recv, at, me, count):
-        for k in range(1, count):
-            remote(buf.at[me], buf.at[me], send.at[k], recv.at[k], at(k)).wait()
+        others = buf.at[pl.ds(0, count - 1)]
+        remote(others, others, send, recv, at(1)).wait()
 
     def on_x(buf, slot):
         return (buf, x_send.at[slot], x_recv.at[slot], at_x, px, NX)
@@ -343,11 +343,8 @@
         collect(*on_r(rbuf.at[1, c], QUARTERS + 2 + c))
         g_out[rows, :] = yn[rows, :] - 0.5 * (lse[rows, :] + jnp.log(add(rbuf.at[1, c], NR, mb // 2)))
 
-    for k in range(NZ):
-        if k:
-            z_copy(k).wait_send()
-        for s in range(1, NX):
-            x_copy(k, s).wait_send()
+    remote(shards(NZ - 1), shards(NZ - 1), gz_send, gz_recv.at[1], at_z(1)).wait_send()
+    remote(shards(NZ * (NX - 1)), shards(NZ * (NX - 1)), gx_send, gx_recv.at[0], at_x(1)).wait_send()
 
 
 def local(logged, targets, log_a, log_b, start_g):
@@ -392,16 +389,16 @@
             pltpu.VMEM((2, 2, NZ, nb // 2, 128), BF16),
             pltpu.VMEM((2, 2, NR, mb // 2, 128), F32),
             dma((5,)),
-            dma((NZ, NX)),
-            dma((NZ, NX)),
+            dma(()),
             dma((NZ,)),
+            dma(()),
             dma((NZ,)),
-            dma((6, NX)),
-            dma((6, NX)),
-            dma((6, NZ)),
-            dma((6, NZ)),
-            dma((QUARTERS + 4, NR)),
-            dma((QUARTERS + 4, NR)),
+            dma((6,)),
+            dma((6,)),
+            dma((6,)),
+            dma((6,)),
+            dma((QUARTERS + 4,)),
+            dma((QUARTERS + 4,)),
         ],
         compiler_params=pltpu.CompilerParams(
             collective_id=0, has_side_effects=True, vmem_limit_bytes=64 * 1024 * 1024

time: 91.8 us -> 88.8 us (0.967)
  Pallas kernels: 89.1 us -> 86 us
    pallas_call x1, Pallas kernels: 89.1 us -> 86 us  [local(): pl.pallas_call(kernel, out_shape=(jax.ShapeDtypeStruct((nb, 128), F32), j...]
where the time goes in v6:
time: 88.8 us; the launch traced here: 88.6 us
  Pallas kernels  86 us (97%)
  local copies, waits for them, and re-layouts  1.93 us (2%)
    pallas_call x1, Pallas kernels, local(): pl.pallas_call(kernel, out_shape=(jax.ShapeDtypeStruct((nb, 128), F32), j...  86 us
    unnamed x4, local copies, waits for them, and re-layouts  1.93 us

profile of v6, /device:TPU:1, one launch (start us, length us, event | category | flops | bytes accessed | tf_op | source)
XLA Modules:
  0.0 88.6 jit_solution(8314055691861463219)
XLA Ops:
  0.6 86.0 %shard_map.68 = (f32[32,128]{1,0:T(8,128)}, f32[16,128]{1,0:T(8,128)}) custom-call(bf16[128,128]{1,0:T(8,128)(2,1)} %x_hbm.1, bf16[2048,128]{1,0:T(8,128)(2,1)} %y_hbm.1, f32[32,128]{1,0:T(8,128)} %bitcast.5, f32[1,2048]{1,0:T(1,128)} %bitcast.7, f32[1,2048]{1,0:T(1,128)} %bitcast.8), custom_call_target="tpu_custom_call" | custom-call | tf_op jit(solution)/shard_map/pallas_call | solution.py:357
  86.7 0.0 copy-start
  86.7 1.3 %copy.9 = f32[4096]{0:T(1024)} copy(f32[4096]{0:T(1024)} %bitcast.6) | data formatting | bytes 32768
  88.0 0.0 copy-done
  88.0 0.6 copy.10
Async XLA Ops:
  86.7 1.3 %copy-start = (f32[16,128]{1,0:T(8,128)S(1)}, f32[16,128]{1,0:T(8,128)}, u32[]{:S(2)}) copy-start(f32[16,128]{1,0:T(8,128)} %get-tuple-element.5) | copy-start | bytes 24580

commit v7 on v6

--- a/solution.py
+++ b/solution.py
@@ -233,7 +233,7 @@
             xn[pl.ds(2 * k + 1, 1), :] = norm[:, 128:256]
             return carry
 
-        lax.fori_loop(0, tiles, one, 0)
+        lax.fori_loop(0, tiles, one, 0, unroll=8)
 
     pack(xpair.at[px], rowstat[0:nb, :], rowstat[nb : 2 * nb, :])
     spread(*on_x(xpair, 0))

time: 88.8 us -> 88.8 us (level)
  no operation moved by 1% of the time
where the time goes in v7:
time: 88.8 us; the launch traced here: 88.6 us
  Pallas kernels  86 us (97%)
  local copies, waits for them, and re-layouts  1.93 us (2%)
    pallas_call x1, Pallas kernels, local(): pl.pallas_call(kernel, out_shape=(jax.ShapeDtypeStruct((nb, 128), F32), j...  86 us
    unnamed x4, local copies, waits for them, and re-layouts  1.93 us

profile of v7, /device:TPU:1, one launch (start us, length us, event | category | flops | bytes accessed | tf_op | source)
XLA Modules:
  0.0 88.6 jit_solution(16205099848818883889)
XLA Ops:
  0.6 86.0 %shard_map.68 = (f32[32,128]{1,0:T(8,128)}, f32[16,128]{1,0:T(8,128)}) custom-call(bf16[128,128]{1,0:T(8,128)(2,1)} %x_hbm.1, bf16[2048,128]{1,0:T(8,128)(2,1)} %y_hbm.1, f32[32,128]{1,0:T(8,128)} %bitcast.5, f32[1,2048]{1,0:T(1,128)} %bitcast.7, f32[1,2048]{1,0:T(1,128)} %bitcast.8), custom_call_target="tpu_custom_call" | custom-call | tf_op jit(solution)/shard_map/pallas_call | solution.py:357
  86.7 0.0 copy-start
  86.7 1.3 %copy.9 = f32[4096]{0:T(1024)} copy(f32[4096]{0:T(1024)} %bitcast.6) | data formatting | bytes 32768
  88.0 0.0 copy-done
  88.0 0.6 copy.10
Async XLA Ops:
  86.7 1.3 %copy-start = (f32[16,128]{1,0:T(8,128)S(1)}, f32[16,128]{1,0:T(8,128)}, u32[]{:S(2)}) copy-start(f32[16,128]{1,0:T(8,128)} %get-tuple-element.5) | copy-start | bytes 24580
